TPU v7x, 32 devices: a whole 2x2x4 slice. The times are simulated.
32 devices in a mesh: mem: 8 (over z, y), reg: 4 (over x, core).
Axes of the slice: x: 2, y: 2, z: 4, core: 2. Of those that a mesh axis runs over, the one named last changes fastest.
Arguments:
- prior_tracer_draws: float32 [8, 32, 2048], P('mem', 'reg'), may hold values from -6 to 6
- courant_row: bfloat16 [32, 2048], P('reg'), may hold values from -0.25 to 0.25
- courant_column: bfloat16 [32, 2048], P('reg'), may hold values from -0.25 to 0.25
- diffusion: bfloat16 [32, 2048], P('reg'), may hold values from 0.049804688 to 0.19921875
- obs_value: float32 [128], replicated, may hold values from -6 to 6
- observation_variance: float32 [128], replicated, may hold values from 0.25 to 1
- obs_noise: float32 [128, 8], replicated, may hold values from -5 to 5
- obs_owner: int32 [128], replicated, may hold values from 0 to 31
- obs_cell: int32 [128], replicated, may hold values from 0 to 2047
- obs_order: int32 [128], replicated, may hold values from 0 to 127, each once
Outputs:
- posterior_tracer_draws: float32 [8, 32, 2048], P('mem', 'reg')
Inputs may be any that keep to these rules, and one draw needn't show every extreme that they name: `obs_owner`: numbers a slab as its index along mem times the size of reg plus its index along reg; slab (p, r) holds rows r * 8 + p * 1 to r * 8 + (p + 1) - 1. `obs_cell`: row-major cell within the slab's 1 x 2048 cells. `obs_order`: each observation once.
All inputs are finite; a program needn't handle non-finite values.
Results may differ from a plain program's by a relative error of at most 0.0003.
Values may be sent and summed in bfloat16 or wider, within the bound.
No kernel may reach another device: no remote copies, remote signals or barrier semaphores. Data moves between devices by JAX's collectives and lax.ppermute only.
A program may use at most 64 MiB of HBM per device.

v0:
```python
import jax
import jax.numpy as jnp
from jax import lax
from jax.sharding import PartitionSpec as P

NOB = 64
NBLK = 2


HIGH = lax.Precision.HIGHEST


def extended(cells, sides, width):
    for axis, dim in sides:
        count = lax.axis_size(axis)
        head = lax.slice_in_dim(cells, 0, width, axis=dim)
        tail = lax.slice_in_dim(cells, cells.shape[dim] - width, cells.shape[dim], axis=dim)
        cells = jnp.concatenate(
            [
                lax.ppermute(tail, axis, [(i, (i + 1) % count) for i in range(count)]),
                cells,
                lax.ppermute(head, axis, [((i + 1) % count, i) for i in range(count)]),
            ],
            axis=dim,
        )
    return cells


def bell(delta, period, scale):
    delta = delta % period
    dist = jnp.minimum(delta, period - delta).astype(jnp.float32)
    return jnp.exp(-0.5 * (dist / scale) ** 2)


def advance_rows(haloed_extended_grid, courant_row, courant_column, diffusion):
    centre = haloed_extended_grid[1:-1]
    north = haloed_extended_grid[:-2]
    south = haloed_extended_grid[2:]
    west = jnp.roll(centre, 1, axis=1)
    east = jnp.roll(centre, -1, axis=1)
    return (
        centre
        - 0.5 * courant_column * (east - west)
        - 0.5 * courant_row * (south - north)
        + diffusion * (north + south + east + west - 4.0 * centre)
    )


def measured_kalman_gain(prior, values, variance, noise):
    members = prior.shape[0]
    anomaly = prior - jnp.mean(prior, axis=0)
    spread = jnp.dot(anomaly.T, anomaly, precision=HIGH, preferred_element_type=jnp.float32) / (
        members - 1
    )
    system = spread + jnp.diag(variance)
    factor = jnp.linalg.cholesky(system)
    innovation = values[:, None] + jnp.sqrt(variance)[:, None] * noise - prior.T
    weights = jax.scipy.linalg.cho_solve((factor, True), innovation)
    return (anomaly, weights)


def increment(columns, anomaly, weights, taper):
    members = columns.shape[0]
    centred = columns - jnp.mean(columns, axis=0)
    cross = lax.dot_general(
        centred,
        anomaly,
        (((0,), (0,)), ((), ())),
        precision=HIGH,
        preferred_element_type=jnp.float32,
    ) / (members - 1)
    return columns + lax.dot_general(
        weights,
        taper * cross,
        (((0,), (1,)), ((), ())),
        precision=HIGH,
        preferred_element_type=jnp.float32,
    )


def on_device(
    prior_tracer_draws,
    courant_row,
    courant_column,
    diffusion,
    obs_value,
    observation_variance,
    obs_noise,
    obs_owner,
    obs_cell,
    obs_order,
):
    region_rows = prior_tracer_draws.shape[1]
    columns = prior_tracer_draws.shape[2]
    mem_count = lax.axis_size("mem")
    reg_count = lax.axis_size("reg")
    slab_rows = region_rows // mem_count
    grid_rows = region_rows * reg_count
    latitude_weighting = region_rows // 2
    col_scale = columns // 4
    rate_row = courant_row.astype(jnp.float32)
    column_rate = courant_column.astype(jnp.float32)
    rate_diff = diffusion.astype(jnp.float32)
    field = prior_tracer_draws[0]
    for step in range(2):
        haloed_extended_grid = extended(field, (("reg", 0),), 1)
        field = advance_rows(haloed_extended_grid, rate_row, column_rate, rate_diff)
    slabs = lax.all_to_all(field[None], "mem", split_axis=1, concat_axis=0, tiled=True)
    members = slabs.shape[0]
    cells = slabs.reshape(members, slab_rows * columns)
    me_mem = lax.axis_index("mem")
    me_reg = lax.axis_index("reg")
    myself = me_mem * reg_count + me_reg
    owned_rows = me_reg * region_rows + me_mem * slab_rows + jnp.arange(slab_rows, dtype=jnp.int32)
    obs_row = (
        obs_owner % reg_count * region_rows
        + obs_owner // reg_count * slab_rows
        + obs_cell // columns
    )
    observation_column = obs_cell % columns
    col_index = jnp.arange(columns, dtype=jnp.int32)
    owners = obs_owner[obs_order]
    spots = obs_cell[obs_order]
    sorted_row = obs_row[obs_order]
    sorted_col = observation_column[obs_order]
    local = jnp.where((owners == myself)[None, :], cells[:, spots], 0.0)
    priors = lax.psum(local, ("mem", "reg"))
    for block in range(NBLK):
        lower = block * NOB
        upper = (block + 1) * NOB
        chosen = obs_order[lower:upper]
        prior = priors[:, lower:upper]
        anomaly, weights = measured_kalman_gain(
            prior, obs_value[chosen], observation_variance[chosen], obs_noise[chosen]
        )
        orow = sorted_row[lower:upper]
        ocol = sorted_col[lower:upper]
        row_taper = bell(owned_rows[:, None] - orow[None, :], grid_rows, latitude_weighting)
        col_taper = bell(col_index[:, None] - ocol[None, :], columns, col_scale)
        cells = increment(
            cells,
            anomaly,
            weights,
            (row_taper[:, None, :] * col_taper[None, :, :]).reshape(
                slab_rows * columns, orow.shape[0]
            ),
        )
        obs_taper = bell(sorted_row[:, None] - orow[None, :], grid_rows, latitude_weighting) * bell(
            sorted_col[:, None] - ocol[None, :], columns, col_scale
        )
        priors = increment(priors, anomaly, weights, obs_taper)
    return lax.all_to_all(
        cells.reshape(members, slab_rows, columns), "mem", split_axis=0, concat_axis=1, tiled=True
    )


def solution(mesh):
    placed = (
        P("mem", "reg", None),
        P("reg", None),
        P("reg", None),
        P("reg", None),
        P(),
        P(),
        P(),
        P(),
        P(),
        P(),
    )
    return jax.shard_map(
        on_device, mesh=mesh, in_specs=placed, out_specs=P("mem", "reg", None), check_vma=False
    )
```

profile of v0, /device:TPU:0, one launch (start us, length us, event | category | flops | bytes accessed | tf_op | source)
XLA Modules:
  0.0 110.8 jit_solution(9856466728863007897)
XLA Ops:
  0.0 0.9 slice_bitcast_fusion
  0.9 2.5 %collective-permute-start = (f32[1,2048]{1,0:T(1,128)S(1)}, f32[1,2048]{1,0:T(1,128)S(1)}, u32[]{:S(2)}, u32[]{:S(2)}) collective-permute-start(f32[1,2048]{1,0:T(1,128)S(1)} %get-tuple-element.18), channel_id=1, source_target_pairs={{1,0},{2,1},{3,2},{0,3},{5,4},{6,5},{7,6},{4,7},{9,8},{10,9},{11,1... | collective-permute-start | bytes 24584 | tf_op jit(solution)/shard_map/ppermute | solution.py:22
  3.4 1.0 fusion.103
  5.8 1.2 %gather_fusion.1 = s32[128]{0:T(128)S(1)} fusion(s32[128]{0:T(128)S(1)} %copy-done.2, s32[1024]{0:T(1024)S(1)} %pad_clamp_fusion.3), kind=kCustom, calls=%fused_computation.1 | custom fusion | bytes 1536 | tf_op jit(solution)/shard_map/gather | solution.py:123
  7.1 1.2 %gather_fusion = s32[128]{0:T(128)S(1)} fusion(s32[128]{0:T(128)S(1)} %copy-done.3, s32[1024]{0:T(1024)S(1)} %pad_clamp_fusion.3), kind=kCustom, calls=%fused_computation | custom fusion | bytes 1536 | tf_op jit(solution)/shard_map/gather | solution.py:122
  8.4 1.2 %gather_fusion.7 = s32[128]{0:T(128)S(1)} fusion(s32[128]{0:T(128)S(1)} %get-tuple-element.26, s32[1024]{0:T(1024)S(1)} %pad_clamp_fusion.3), kind=kCustom, calls=%fused_computation.7 | custom fusion | bytes 1536 | tf_op jit(solution)/shard_map/gather | solution.py:125
  9.7 1.2 %gather_fusion.6 = s32[128]{0:T(128)S(1)} fusion(s32[128]{0:T(128)S(1)} %get-tuple-element.25, s32[1024]{0:T(1024)S(1)} %pad_clamp_fusion.3), kind=kCustom, calls=%fused_computation.6 | custom fusion | bytes 1536 | tf_op jit(solution)/shard_map/gather | solution.py:124
  11.3 1.8 %collective-permute-start.2 = (f32[1,2048]{1,0:T(1,128)S(1)}, f32[1,2048]{1,0:T(1,128)S(1)}, u32[]{:S(2)}, u32[]{:S(2)}) collective-permute-start(f32[1,2048]{1,0:T(1,128)S(1)} %get-tuple-element.12), channel_id=1, source_target_pairs={{1,0},{2,1},{3,2},{0,3},{5,4},{6,5},{7,6},{4,7},{9,8},{10,9},{11,1... | collective-permute-start | bytes 24584 | tf_op jit(solution)/shard_map/ppermute | solution.py:22
  13.2 1.3 %collective-permute-done.2 = f32[1,2048]{1,0:T(1,128)S(1)} collective-permute-done((f32[1,2048]{1,0:T(1,128)S(1)}, f32[1,2048]{1,0:T(1,128)S(1)}, u32[]{:S(2)}, u32[]{:S(2)}) %collective-permute-start.2) | collective-permute-done | bytes 8224 | tf_op jit(solution)/shard_map/ppermute | solution.py:22
  14.5 1.7 %collective-permute-done.3 = f32[1,2048]{1,0:T(1,128)S(1)} collective-permute-done((f32[1,2048]{1,0:T(1,128)S(1)}, f32[1,2048]{1,0:T(1,128)S(1)}, u32[]{:S(2)}, u32[]{:S(2)}) %collective-permute-start.3) | collective-permute-done | bytes 8224 | tf_op jit(solution)/shard_map/ppermute | solution.py:20
  17.0 5.8 %all-to-all-start = ((f32[1,8,2048]{2,0,1:T(1,128)}), f32[1,8,2048]{2,0,1:T(1,128)S(1)}, u32[]{:S(2)}, u32[]{:S(2)}) async-start(f32[1,8,2048]{2,0,1:T(1,128)} %broadcast_in_dim.46), calls=%async_computation | async-start | bytes 131072 | tf_op jit(solution)/shard_map/all_to_all | solution.py:108
  23.6 0.8 gather_fusion.3
  25.0 0.8 gather_fusion.8
  26.4 0.8 gather_fusion.4
  27.2 0.8 gather_fusion.9
  28.1 1.6 %all-to-all-done = f32[1,8,2048]{2,0,1:T(1,128)S(1)} async-done(((f32[1,8,2048]{2,0,1:T(1,128)}), f32[1,8,2048]{2,0,1:T(1,128)S(1)}, u32[]{:S(2)}, u32[]{:S(2)}) %all-to-all-start) | async-done | bytes 65568 | tf_op jit(solution)/shard_map/all_to_all | solution.py:108
  30.8 38.3 %psum.7 = f32[8,128]{1,0:T(8,128)S(1)} all-reduce(f32[8,128]{1,0:T(8,128)S(1)} %select_bitcast_fusion), channel_id=1, replica_groups=mesh['mem'=8,'reg'=4] {'mem','reg'}, use_global_device_ids=true, to_apply=%region_0.1 | all-reduce | flops 1024 | bytes 8192 | tf_op jit(solution)/shard_map/psum | solution.py:127
  69.5 5.8 %cholesky.44 = f32[64,64]{1,0:T(8,128)S(1)} custom-call(f32[64,64]{1,0:T(8,128)S(1)} %fusion.54), custom_call_target="Cholesky" | custom-call | tf_op jit(solution)/shard_map/jit(cholesky)/cholesky | solution.py:56
  76.7 4.9 %custom-call.8 = f32[1,64,64]{1,2,0:T(8,128)S(1)} custom-call(f32[1,64,64]{2,1,0:T(8,128)S(1)} %fusion.30), custom_call_target="InvertDiagBlocksLowerTriangular" | custom-call | tf_op jit(solution)/shard_map/jit(_cho_solve)/triangular_solve | solution.py:58
  82.4 0.9 fusion.1
  84.2 5.8 %cholesky.55 = f32[64,64]{1,0:T(8,128)S(1)} custom-call(f32[64,64]{1,0:T(8,128)S(1)} %fusion.49), custom_call_target="Cholesky" | custom-call | tf_op jit(solution)/shard_map/jit(cholesky)/cholesky | solution.py:56
  91.4 4.9 %custom-call.9 = f32[1,64,64]{1,2,0:T(8,128)S(1)} custom-call(f32[1,64,64]{2,1,0:T(8,128)S(1)} %fusion.31), custom_call_target="InvertDiagBlocksLowerTriangular" | custom-call | tf_op jit(solution)/shard_map/jit(_cho_solve)/triangular_solve | solution.py:58
  96.7 1.0 fusion
  98.2 12.0 %all_to_all.21 = f32[8,1,2048]{2,1,0:T(1,128)S(1)} all-to-all(f32[8,1,2048]{2,1,0:T(1,128)S(1)} %copy.41), channel_id=1, replica_groups=mesh['mem'=8,'reg'=4] {'mem'}, dimensions={0} | all-to-all | bytes 131072 | tf_op jit(solution)/shard_map/all_to_all | solution.py:152
  (83 shorter events, 12.1 us)
Async XLA Ops:
  0.0 23.6 %copy-start = (f32[128]{0:T(128)S(1)}, f32[128]{0:T(128)}, u32[]{:S(2)}) copy-start(f32[128]{0:T(128)} %param.18) | copy-start | bytes 1540
  0.9 10.1 %collective-permute-start = (f32[1,2048]{1,0:T(1,128)S(1)}, f32[1,2048]{1,0:T(1,128)S(1)}, u32[]{:S(2)}, u32[]{:S(2)}) collective-permute-start(f32[1,2048]{1,0:T(1,128)S(1)} %get-tuple-element.18), channel_id=1, source_target_pairs={{1,0},{2,1},{3,2},{0,3},{5,4},{6,5},{7,6},{4,7},{9,8},{10,9},{11,1... | collective-permute-start | bytes 24584 | tf_op jit(solution)/shard_map/ppermute | solution.py:22
  3.4 7.7 %collective-permute-start.1 = (f32[1,2048]{1,0:T(1,128)S(1)}, f32[1,2048]{1,0:T(1,128)S(1)}, u32[]{:S(2)}, u32[]{:S(2)}) collective-permute-start(f32[1,2048]{1,0:T(1,128)S(1)} %get-tuple-element.17), channel_id=1, source_target_pairs={{0,1},{1,2},{2,3},{3,0},{4,5},{5,6},{6,7},{7,4},{8,9},{9,10},{10,1... | collective-permute-start | bytes 24584 | tf_op jit(solution)/shard_map/ppermute | solution.py:20
  3.4 1.0 copy-start.4
  4.5 0.7 copy-start.9
  5.2 0.7 copy-start.2
  5.8 1.2 %copy-start.3 = (s32[128]{0:T(128)S(1)}, s32[128]{0:T(128)}, u32[]{:S(2)}) copy-start(s32[128]{0:T(128)} %param.20) | copy-start | bytes 1540
  9.7 1.4 %copy-start.5 = (bf16[8,2048]{1,0:T(8,128)(2,1)S(1)}, bf16[8,2048]{1,0:T(8,128)(2,1)}, u32[]{:S(2)}) copy-start(bf16[8,2048]{1,0:T(8,128)(2,1)} %param.16) | copy-start | bytes 98308
  9.7 1.4 %copy-start.6 = (bf16[8,2048]{1,0:T(8,128)(2,1)S(1)}, bf16[8,2048]{1,0:T(8,128)(2,1)}, u32[]{:S(2)}) copy-start(bf16[8,2048]{1,0:T(8,128)(2,1)} %param.14) | copy-start | bytes 98308
  9.7 1.4 %copy-start.7 = (bf16[8,2048]{1,0:T(8,128)(2,1)S(1)}, bf16[8,2048]{1,0:T(8,128)(2,1)}, u32[]{:S(2)}) copy-start(bf16[8,2048]{1,0:T(8,128)(2,1)} %param.15) | copy-start | bytes 98308
  11.3 3.2 %collective-permute-start.2 = (f32[1,2048]{1,0:T(1,128)S(1)}, f32[1,2048]{1,0:T(1,128)S(1)}, u32[]{:S(2)}, u32[]{:S(2)}) collective-permute-start(f32[1,2048]{1,0:T(1,128)S(1)} %get-tuple-element.12), channel_id=1, source_target_pairs={{1,0},{2,1},{3,2},{0,3},{5,4},{6,5},{7,6},{4,7},{9,8},{10,9},{11,1... | collective-permute-start | bytes 24584 | tf_op jit(solution)/shard_map/ppermute | solution.py:22
  13.1 3.1 %collective-permute-start.3 = (f32[1,2048]{1,0:T(1,128)S(1)}, f32[1,2048]{1,0:T(1,128)S(1)}, u32[]{:S(2)}, u32[]{:S(2)}) collective-permute-start(f32[1,2048]{1,0:T(1,128)S(1)} %get-tuple-element.11), channel_id=1, source_target_pairs={{0,1},{1,2},{2,3},{3,0},{4,5},{5,6},{6,7},{7,4},{8,9},{9,10},{10,1... | collective-permute-start | bytes 24584 | tf_op jit(solution)/shard_map/ppermute | solution.py:20
  17.0 12.7 %all-to-all-start = ((f32[1,8,2048]{2,0,1:T(1,128)}), f32[1,8,2048]{2,0,1:T(1,128)S(1)}, u32[]{:S(2)}, u32[]{:S(2)}) async-start(f32[1,8,2048]{2,0,1:T(1,128)} %broadcast_in_dim.46), calls=%async_computation | async-start | bytes 131072 | tf_op jit(solution)/shard_map/all_to_all | solution.py:108
  22.8 0.7 copy-start.8
  25.7 0.7 copy-start.1
where the time goes:
time: 111 us
  blocking collectives  50.3 us (45%)
  other arithmetic  24.8 us (22%)
  local copies, waits for them, and re-layouts  16.3 us (15%)
  starting transfers between devices  10.1 us (9%)
  waiting for transfers between devices  4.59 us (4%)
  matrix products  4.37 us (4%)
    psum x1, blocking collectives, on_device(): priors = lax.psum(local, ('mem', 'reg'))  38.3 us
    another operation x6, other arithmetic, measured_kalman_gain(): factor = jnp.linalg.cholesky(system)  13 us
    all_to_all x1, blocking collectives, on_device(): lax.all_to_all(cells.reshape(members, slab_rows, columns), 'mem', split_a...  12 us
    another operation x4, other arithmetic, measured_kalman_gain(): weights = jax.scipy.linalg.cho_solve((factor, True), innovation)  11.1 us
    all_to_all x1, starting transfers between devices, on_device(): lax.all_to_all(field[None], 'mem', split_axis=1, concat_axis=0, tiled=True)  5.84 us
    ppermute x2, starting transfers between devices, extended(): lax.ppermute(head, axis, [((i + 1) % count, i) for i in range(count)])  4.25 us
    unnamed x22, local copies, waits for them, and re-layouts  2.49 us
    dot_general x3, matrix products, increment(): lax.dot_general(centred, anomaly, (((0,), (0,)), ((), ())), precision=HIG...  2.26 us
  transfers between devices with their start and end apart: 5, of which 3 were waited for; matrix products, arithmetic and copies ran while one was open for 10% of the time, Pallas kernels for 0%

commit v1 on v0

--- a/solution.py
+++ b/solution.py
@@ -1,6 +1,10 @@
+import functools
+
 import jax
 import jax.numpy as jnp
 from jax import lax
+from jax.experimental import pallas as pl
+from jax.experimental.pallas import tpu as pltpu
 from jax.sharding import PartitionSpec as P
 
 NOB = 64
@@ -78,7 +82,7 @@
     )
 
 
-def on_device(
+def on_slabs(
     prior_tracer_draws,
     courant_row,
     courant_column,
@@ -154,6 +158,483 @@
     )
 
 
+SUBLANES = 8
+LANES = 128
+POINTS = [(dr, dc) for dr in range(-2, 3) for dc in range(-2, 3) if abs(dr) + abs(dc) <= 2]
+CROSS = [(0, 0), (-1, 0), (1, 0), (0, -1), (0, 1)]
+TILES = -(-(len(POINTS) + 3 * len(CROSS)) // SUBLANES)
+PARTS = 4
+
+
+def iota(axis, shape=(SUBLANES, LANES)):
+    return lax.broadcasted_iota(jnp.int32, shape, axis)
+
+
+def row_of(x, i):
+    return jnp.broadcast_to(x[i : i + 1, :], x.shape)
+
+
+def stencil(q, north, south, rate_row, rate_col, rate_diff):
+    columns = q.shape[1]
+    west = pltpu.roll(q, 1, axis=1)
+    east = pltpu.roll(q, columns - 1, axis=1)
+    return (
+        q
+        - 0.5 * rate_col * (east - west)
+        - 0.5 * rate_row * (south - north)
+        + rate_diff * (north + south + east + west - 4.0 * q)
+    )
+
+
+def slot(c):
+    return c % SUBLANES, c // SUBLANES * LANES
+
+
+def start_kernel(
+    sizes,
+    q_ref,
+    row_ref,
+    col_ref,
+    diff_ref,
+    owner_ref,
+    cell_ref,
+    order_ref,
+    value_ref,
+    variance_ref,
+    noise_ref,
+    down_ref,
+    up_ref,
+    points_ref,
+    partial_ref,
+    sorted_ref,
+    noise_out,
+):
+    reg_count, region_rows, slab_rows, columns = sizes
+    grid_rows = reg_count * region_rows
+    packed = columns // SUBLANES
+    me = lax.axis_index("reg")
+    sub = iota(0)
+    owner = owner_ref[...]
+    cell = cell_ref[...]
+    shift = columns.bit_length() - 1
+    obs_row = (
+        (owner & (reg_count - 1)) * region_rows
+        + (owner >> (reg_count.bit_length() - 1)) * slab_rows
+        + (cell >> shift)
+    )
+    obs_col = cell & (columns - 1)
+    table = jnp.where(
+        sub == 0,
+        obs_row.astype(jnp.float32),
+        jnp.where(
+            sub == 1,
+            obs_col.astype(jnp.float32),
+            jnp.where(sub == 2, value_ref[...], jnp.where(sub == 3, variance_ref[...], 0.0)),
+        ),
+    )
+    square = (LANES, LANES)
+    pick = (iota(0, square) == order_ref[...]).astype(jnp.float32)
+    both = jnp.dot(
+        jnp.concatenate([table, noise_ref[...]], axis=0),
+        pick,
+        precision=HIGH,
+        preferred_element_type=jnp.float32,
+    )
+    table = both[:SUBLANES]
+    sorted_ref[...] = table
+    noise_out[...] = both[SUBLANES:]
+    orow = row_of(table, 0).astype(jnp.int32)
+    ocol = row_of(table, 1).astype(jnp.int32)
+
+    q = q_ref[0]
+    rates = [r[...].astype(jnp.float32) for r in (row_ref, col_ref, diff_ref)]
+    local_row = orow - me * region_rows
+    for dc in range(-2, 3):
+        index = (ocol + dc) & (columns - 1)
+        lane = index & (LANES - 1)
+        tile = index >> (LANES.bit_length() - 1)
+        wanted = [(q, 0, POINTS)]
+        if abs(dc) <= 1:
+            for n, rate in enumerate(rates):
+                wanted.append((rate, len(POINTS) + n * len(CROSS), CROSS))
+        hits = [tile == t for t in range(columns // LANES)]
+        for array, base, points in wanted:
+            found = jnp.zeros((SUBLANES, LANES), jnp.float32)
+            for t in range(columns // LANES):
+                taken = jnp.take_along_axis(
+                    array[:, t * LANES : (t + 1) * LANES], lane, axis=1, mode="promise_in_bounds"
+                )
+                found = jnp.where(hits[t], taken, found)
+            for n, (dr, shift_col) in enumerate(points):
+                if shift_col != dc:
+                    continue
+                here = ((local_row + dr) & (grid_rows - 1)) == sub
+                s, at = slot(base + n)
+                points_ref[s : s + 1, at : at + LANES] = jnp.sum(
+                    jnp.where(here, found, 0.0), axis=0, keepdims=True
+                )
+    for c in range(len(POINTS) + 3 * len(CROSS), TILES * SUBLANES):
+        s, at = slot(c)
+        points_ref[s : s + 1, at : at + LANES] = jnp.zeros((1, LANES), jnp.float32)
+
+    rate_row, rate_col, rate_diff = rates
+    wide = iota(0, (SUBLANES, columns))
+    north = jnp.where(wide == 0, 0.0, pltpu.roll(q, 1, axis=0))
+    south = jnp.where(wide == SUBLANES - 1, 0.0, pltpu.roll(q, SUBLANES - 1, axis=0))
+    partial = stencil(q, north, south, rate_row, rate_col, rate_diff)
+    partial_ref[...] = partial
+    for ref, edge, missing in (
+        (down_ref, SUBLANES - 1, rate_diff - 0.5 * rate_row),
+        (up_ref, 0, rate_diff + 0.5 * rate_row),
+    ):
+        for n, array in enumerate((q, partial, missing)):
+            for s in range(SUBLANES):
+                ref[s : s + 1, n * packed : (n + 1) * packed] = array[
+                    edge : edge + 1, s * packed : (s + 1) * packed
+                ]
+        ref[:, 3 * packed :] = points_ref[...]
+
+
+def bell_of(dist, period, scale):
+    dist = jnp.abs(dist)
+    dist = jnp.minimum(dist, period - dist) / scale
+    return jnp.exp(-0.5 * (dist * dist))
+
+
+def halves(x):
+    high = x.astype(jnp.bfloat16)
+    return high, (x - high.astype(jnp.float32)).astype(jnp.bfloat16)
+
+
+def taper_kernel(sizes, sorted_ref, columns_ref, obs_ref, rows_ref):
+    reg_count, region_rows, slab_rows, columns = sizes
+    width = columns // PARTS
+    grid_rows = reg_count * region_rows
+    row_scale, col_scale = float(region_rows // 2), float(columns // 4)
+    part = lax.axis_index("mem") % PARTS
+    me = lax.axis_index("reg")
+    square = (LANES, LANES)
+    row_lanes = jnp.broadcast_to(sorted_ref[0:1, :], square)
+    col_lanes = jnp.broadcast_to(sorted_ref[1:2, :], square)
+    row_subs = row_lanes.T
+    col_subs = col_lanes.T
+    for t in range(width // LANES):
+        at = (part * width + t * LANES + iota(1, square)).astype(jnp.float32)
+        high, low = halves(bell_of(at - col_subs, float(columns), col_scale))
+        columns_ref[0, :, t * LANES : (t + 1) * LANES] = high
+        columns_ref[1, :, t * LANES : (t + 1) * LANES] = low
+    high, low = halves(
+        bell_of(row_lanes - row_subs, float(grid_rows), row_scale)
+        * bell_of(col_lanes - col_subs, float(columns), col_scale)
+    )
+    obs_ref[0] = high
+    obs_ref[1] = low
+    rows = (me * region_rows + iota(0)).astype(jnp.float32)
+    rows_ref[...] = bell_of(rows - row_lanes[:SUBLANES], float(grid_rows), row_scale)
+
+
+def middle_kernel(
+    sizes,
+    partial_ref,
+    row_ref,
+    col_ref,
+    diff_ref,
+    down_ref,
+    up_ref,
+    points_ref,
+    above_ref,
+    below_ref,
+    far_ref,
+    out_ref,
+    edge_ref,
+):
+    reg_count, region_rows, slab_rows, columns = sizes
+    packed = columns // SUBLANES
+    width = columns // PARTS
+    wide = iota(0, (SUBLANES, columns))
+    rate_row, rate_col, rate_diff = [
+        r[...].astype(jnp.float32) for r in (row_ref, col_ref, diff_ref)
+    ]
+
+    def section(ref, n):
+        return ref[:, n * packed : (n + 1) * packed]
+
+    outer = (
+        section(above_ref, 0),
+        section(below_ref, 0),
+        section(above_ref, 1) + section(above_ref, 2) * section(up_ref, 0),
+        section(below_ref, 1) + section(below_ref, 2) * section(down_ref, 0),
+    )
+    for n, array in enumerate(outer):
+        for s in range(SUBLANES):
+            edge_ref[n : n + 1, s * packed : (s + 1) * packed] = array[s : s + 1, :]
+
+    def edge(n):
+        return jnp.broadcast_to(edge_ref[n : n + 1, :], (SUBLANES, columns))
+
+    first, last = wide == 0, wide == SUBLANES - 1
+    field = (
+        partial_ref[...]
+        + jnp.where(first, (rate_diff + 0.5 * rate_row) * edge(0), 0.0)
+        + jnp.where(last, (rate_diff - 0.5 * rate_row) * edge(1), 0.0)
+    )
+    north = jnp.where(first, edge(2), pltpu.roll(field, 1, axis=0))
+    south = jnp.where(last, edge(3), pltpu.roll(field, SUBLANES - 1, axis=0))
+    field = stencil(field, north, south, rate_row, rate_col, rate_diff)
+
+    points = points_ref[...] + far_ref[...] + above_ref[:, 3 * packed :] + below_ref[:, 3 * packed :]
+
+    def point(c):
+        s, at = slot(c)
+        return points[s : s + 1, at : at + LANES]
+
+    q0 = {p: point(n) for n, p in enumerate(POINTS)}
+    rates = [
+        {p: point(len(POINTS) + n * len(CROSS) + i) for i, p in enumerate(CROSS)} for n in range(3)
+    ]
+
+    def at_point(values, p):
+        i, j = p
+        here = values[p]
+        north, south = values[i - 1, j], values[i + 1, j]
+        west, east = values[i, j - 1], values[i, j + 1]
+        return (
+            here
+            - 0.5 * rates[1][p] * (east - west)
+            - 0.5 * rates[0][p] * (south - north)
+            + rates[2][p] * (north + south + east + west - 4.0 * here)
+        )
+
+    q1 = {p: at_point(q0, p) for p in CROSS}
+    seen = jnp.broadcast_to(at_point(q1, (0, 0)), (SUBLANES, LANES))
+    for d in range(out_ref.shape[0]):
+        g = d % PARTS
+        out_ref[d, :, :width] = field[:, g * width : (g + 1) * width]
+        out_ref[d, :, width:] = seen
+
+
+def gain(anomaly, precision, innovation):
+    members = anomaly.shape[0]
+    sub = iota(0)
+    weighted = anomaly * precision
+
+    def against(x):
+        total = jnp.sum(weighted * x, axis=1, keepdims=True)
+        return jnp.broadcast_to(total, weighted.shape)
+
+    system = [
+        against(row_of(anomaly, b)) + jnp.where(sub == b, float(members - 1), 0.0)
+        for b in range(members)
+    ]
+    load = [against(row_of(innovation, m)) for m in range(members)]
+    held = anomaly
+    for k in range(members):
+        inverse = 1.0 / row_of(system[k], k)
+        mine = sub == k
+
+        def step(x, k=k, inverse=inverse, mine=mine):
+            scaled = row_of(x, k) * inverse
+            return jnp.where(mine, scaled, x - system[k] * scaled)
+
+        held = step(held)
+        for b in range(k + 1, members):
+            system[b] = step(system[b])
+    fitted = jnp.zeros_like(anomaly)
+    for m in range(members):
+        total = jnp.sum(load[m] * held, axis=0, keepdims=True)
+        fitted = jnp.where(sub == m, jnp.broadcast_to(total, held.shape), fitted)
+    return precision * (innovation - fitted)
+
+
+def twice(x, block):
+    lane = iota(1)
+    half = LANES // 2
+    return jnp.where(lane // half == block, x, pltpu.roll(x, half, axis=1))
+
+
+def weigh(rows, table_ref, block):
+    half = LANES // 2
+    lane = iota(1, rows.shape)
+    high = rows.astype(jnp.bfloat16).astype(jnp.float32)
+    left = jnp.where(lane < half, high, rows - high).astype(jnp.bfloat16)
+    high = table_ref[0, block * half : (block + 1) * half, :]
+    low = table_ref[1, block * half : (block + 1) * half, :]
+    return jnp.dot(
+        jnp.concatenate([left, left], axis=1),
+        jnp.concatenate([high, high, low, low], axis=0),
+        preferred_element_type=jnp.float32,
+    )
+
+
+def finish_kernel(sizes, x_ref, sorted_ref, noise_ref, columns_ref, obs_ref, rows_ref, *outs):
+    reg_count, region_rows, slab_rows, columns = sizes
+    members = x_ref.shape[0]
+    width = columns // PARTS
+    now_ref = outs[-1]
+    outs = outs[:-1]
+    me = lax.axis_index("mem")
+    sub, lane = iota(0), iota(1)
+    half = LANES // 2
+    seen = jnp.zeros((SUBLANES, LANES), jnp.float32)
+    for m in range(members):
+        seen = jnp.where(sub == m, x_ref[m, :, width:], seen)
+    value, variance = row_of(sorted_ref, 2), row_of(sorted_ref, 3)
+    observed = value + jnp.sqrt(variance) * noise_ref[...]
+    inverse_variance = 1.0 / variance
+    scale = 1.0 / (members - 1)
+    current = [x_ref[m, :, :width] for m in range(members)]
+    for block in range(NBLK):
+        anomaly = seen - jnp.sum(seen, axis=0, keepdims=True) * (1.0 / members)
+        precision = jnp.where(lane // half == block, inverse_variance, 0.0)
+        gains = gain(anomaly, precision, observed - seen) * scale
+        gains, local = twice(gains, block), twice(anomaly, block)
+        pairs = [row_of(local, a) * gains for a in range(members)]
+        if block + 1 < NBLK:
+            moved = weigh(jnp.concatenate(pairs, axis=0), obs_ref, block)
+            for a in range(members):
+                seen = seen + row_of(anomaly, a) * moved[a * SUBLANES : (a + 1) * SUBLANES]
+        row_taper = twice(rows_ref[...], block)
+        mean = sum(current[1:], current[0]) * (1.0 / members)
+        centred = [x - mean for x in current]
+        if block + 1 < NBLK:
+            chosen = list(range(members))
+            terms = [
+                [row_taper * row_of(pairs[a], m) for m in chosen] for a in range(members)
+            ]
+            start = current
+        else:
+            for m in range(members):
+                now_ref[m] = current[m]
+            chosen = list(range(PARTS))
+            starts = [now_ref[me ^ x] for x in chosen]
+            terms = []
+            for a in range(members):
+                held = pairs[a]
+                row = []
+                for x in chosen:
+                    mine = jnp.sum(jnp.where(sub == (me ^ x), held, 0.0), axis=0, keepdims=True)
+                    row.append(row_taper * mine)
+                terms.append(row)
+            start = starts
+        weights = weigh(
+            jnp.concatenate([t for row in terms for t in row], axis=0), columns_ref, block
+        )
+        updated = []
+        for n in range(len(chosen)):
+            total = start[n]
+            for a in range(members):
+                at = (a * len(chosen) + n) * SUBLANES
+                total = total + centred[a] * weights[at : at + SUBLANES]
+            updated.append(total)
+        current = updated
+    for ref, x in zip(outs, current):
+        ref[...] = x
+
+
+def join_kernel(columns, *refs):
+    out_ref = refs[-1]
+    width = columns // PARTS
+    me = lax.axis_index("mem")
+    for x, ref in enumerate(refs[:-1]):
+        part = (me ^ x) % PARTS
+        out_ref[0, :, pl.ds(pl.multiple_of(part * width, LANES), width)] = ref[...]
+
+
+def call(kernel, outs, args, scratch=(), cost=None):
+    space = pl.BlockSpec(memory_space=pltpu.VMEM)
+    return pl.pallas_call(
+        kernel,
+        out_shape=[jax.ShapeDtypeStruct(s, d) for s, d in outs],
+        in_specs=[space] * len(args),
+        out_specs=[space] * len(outs),
+        scratch_shapes=list(scratch),
+        cost_estimate=cost,
+    )(*args)
+
+
+def on_tile(
+    prior_tracer_draws,
+    courant_row,
+    courant_column,
+    diffusion,
+    obs_value,
+    observation_variance,
+    obs_noise,
+    obs_owner,
+    obs_cell,
+    obs_order,
+):
+    f32 = jnp.float32
+    region_rows, columns = prior_tracer_draws.shape[1:]
+    members = obs_noise.shape[1]
+    mem_count, reg_count = lax.axis_size("mem"), lax.axis_size("reg")
+    sizes = (reg_count, region_rows, region_rows // mem_count, columns)
+    packed = columns // SUBLANES
+    width = columns // PARTS
+    tile = (SUBLANES, LANES)
+    field = (SUBLANES, columns)
+    points_shape = (SUBLANES, TILES * LANES)
+    message = (SUBLANES, 3 * packed + TILES * LANES)
+    rates = (courant_row, courant_column, diffusion)
+    flat = [x.reshape(1, LANES) for x in (obs_owner, obs_cell, obs_order, obs_value, observation_variance)]
+    down, up, points, partial, table, noise = call(
+        functools.partial(start_kernel, sizes),
+        [(message, f32), (message, f32), (points_shape, f32), (field, f32), (tile, f32), (tile, f32)],
+        (prior_tracer_draws, *rates, *flat, obs_noise.T),
+    )
+
+    def shifted(x, by):
+        return lax.ppermute(x, "reg", [(i, (i + by) % reg_count) for i in range(reg_count)])
+
+    above = shifted(down, 1)
+    below = shifted(up, -1)
+    far = [shifted(points, by) for by in range(2, reg_count - 1)]
+    col_taper, obs_taper, row_taper = call(
+        functools.partial(taper_kernel, sizes),
+        [((2, LANES, width), jnp.bfloat16), ((2, LANES, LANES), jnp.bfloat16), (tile, f32)],
+        (table,),
+        cost=pl.CostEstimate(flops=10 * LANES * width, bytes_accessed=8 * LANES * width, transcendentals=LANES * width),
+    )
+    (send,) = call(
+        functools.partial(middle_kernel, sizes),
+        [((mem_count, SUBLANES, width + LANES), f32)],
+        (partial, *rates, down, up, points, above, below, sum(far[1:], far[0])),
+        scratch=[pltpu.VMEM(field, f32)],
+    )
+    slabs = lax.all_to_all(send, "mem", split_axis=0, concat_axis=0, tiled=True)
+    pieces = call(
+        functools.partial(finish_kernel, sizes),
+        [((SUBLANES, width), f32)] * PARTS,
+        (slabs, table, noise, col_taper, obs_taper, row_taper),
+        scratch=[pltpu.VMEM((members, SUBLANES, width), f32)],
+    )
+    back = [pieces[0]] + [
+        lax.ppermute(pieces[x], "mem", [(i, i ^ x) for i in range(mem_count)]) for x in range(1, PARTS)
+    ]
+    (out,) = call(
+        functools.partial(join_kernel, columns), [(prior_tracer_draws.shape, f32)], back
+    )
+    return out
+
+
+def fits_tile(*shapes):
+    draws, noise = shapes
+    members, region_rows, columns = draws
+    counts = (lax.axis_size("mem"), lax.axis_size("reg"))
+    return (
+        members == 1
+        and noise[1] == counts[0] == region_rows == SUBLANES
+        and noise[0] == NOB * NBLK == LANES
+        and counts[1] == PARTS
+        and columns % (PARTS * LANES) == 0
+        and columns & (columns - 1) == 0
+    )
+
+
+def on_device(*args):
+    return (on_tile if fits_tile(args[0].shape, args[6].shape) else on_slabs)(*args)
+
+
 def solution(mesh):
     placed = (
         P("mem", "reg", None),

time: 111 us -> 36.9 us (0.33)
  blocking collectives: 50.3 us -> 0 us
  other arithmetic: 24.8 us -> 0 us
  local copies, waits for them, and re-layouts: 16.3 us -> 1.87 us
  Pallas kernels: 0 us -> 9.38 us
  waiting for transfers between devices: 4.59 us -> 11 us
  matrix products: 4.37 us -> 0 us
  starting transfers between devices: 10.1 us -> 14.2 us
    psum x1 -> x0, blocking collectives: 38.3 us -> none  [on_device(): priors = lax.psum(local, ('mem', 'reg'))]
    another operation x10 -> x0, other arithmetic: 24.1 us -> none  [the longest x6 13 us: measured_kalman_gain(): factor = jnp.linalg.cholesky(system)]
    all_to_all x1 -> x0, blocking collectives: 12 us -> none  [on_device(): lax.all_to_all(cells.reshape(members, slab_rows, columns), 'mem', split_a...]
    gather x14 -> x0, local copies, waits for them, and re-layouts: 10 us -> none  [the longest x2 1.55 us: on_device(): obs_value[chosen]]
    pallas_call x0 -> x5, Pallas kernels: none -> 9.38 us  [call(): pl.pallas_call(kernel, out_shape=[jax.ShapeDtypeStruct(s, d) for s, d in...]
    all_to_all x1, waiting for transfers between devices: 1.58 us -> 5.94 us  [on_tile(): slabs = lax.all_to_all(send, 'mem', split_axis=0, concat_axis=0, tiled=True)]
    ppermute x4 -> x6, starting transfers between devices: 4.26 us -> 8.25 us  [the longest x3 4.76 us: shifted(): lax.ppermute(x, 'reg', [(i, (i + by) % reg_count) for i in range(reg_coun...]
    dot_general x8 -> x0, matrix products: 3.69 us -> none  [the longest x3 2.26 us: increment(): lax.dot_general(centred, anomaly, (((0,), (0,)), ((), ())), precision=HIG...]
  transfers between devices with their start and end apart: 5 -> 7, of which waited for: 3 -> 5; matrix products, arithmetic and copies ran while one was open for 10% -> 0% of each run, Pallas kernels for 0% -> 4%
where the time goes in v1:
time: 36.9 us; the launch traced here: 36.5 us
  starting transfers between devices  14.2 us (38%)
  waiting for transfers between devices  11 us (30%)
  Pallas kernels  9.38 us (25%)
  local copies, waits for them, and re-layouts  1.87 us (5%)
    pallas_call x5, Pallas kernels, call(): pl.pallas_call(kernel, out_shape=[jax.ShapeDtypeStruct(s, d) for s, d in...  9.38 us
    all_to_all x1, waiting for transfers between devices, on_tile(): slabs = lax.all_to_all(send, 'mem', split_axis=0, concat_axis=0, tiled=True)  5.94 us
    all_to_all x1, starting transfers between devices, on_tile(): slabs = lax.all_to_all(send, 'mem', split_axis=0, concat_axis=0, tiled=True)  5.93 us
    ppermute x3, starting transfers between devices, shifted(): lax.ppermute(x, 'reg', [(i, (i + by) % reg_count) for i in range(reg_coun...  4.76 us
    ppermute x3, starting transfers between devices, on_tile(): lax.ppermute(pieces[x], 'mem', [(i, i ^ x) for i in range(mem_count)])  3.49 us
    ppermute x3, waiting for transfers between devices, on_tile(): lax.ppermute(pieces[x], 'mem', [(i, i ^ x) for i in range(mem_count)])  2.7 us
    ppermute x3, waiting for transfers between devices, shifted(): lax.ppermute(x, 'reg', [(i, (i + by) % reg_count) for i in range(reg_coun...  2.37 us
    unnamed x14, local copies, waits for them, and re-layouts  1.87 us
  transfers between devices with their start and end apart: 7, of which 5 were waited for; matrix products, arithmetic and copies ran while one was open for 0% of the time, Pallas kernels for 4%

profile of v1, /device:TPU:0, one launch (start us, length us, event | category | flops | bytes accessed | tf_op | source)
XLA Modules:
  0.0 36.5 jit_solution(857409963425109890)
XLA Ops:
  0.0 2.0 %shard_map.100 = (f32[8,1280]{1,0:T(8,128)}, f32[8,1280]{1,0:T(8,128)}, f32[8,512]{1,0:T(8,128)}, f32[8,2048]{1,0:T(8,128)}, f32[8,128]{1,0:T(8,128)}, /*index=5*/f32[8,128]{1,0:T(8,128)}) custom-call(f32[1,8,2048]{2,1,0:T(8,128)} %q_ref.1, bf16[8,2048]{1,0:T(8,128)(2,1)} %row_ref.3, bf16[8,2048]{1,0:T(8,128)(2,1)} %col_ref.3, bf16[8,2048]{1,0:T(8,128)(2,1)} %diff_ref.3, ...), custom_call_target="tpu_custom_call" | custom-call | tf_op jit(solution)/shard_map/pallas_call | solution.py:545
  2.0 0.5 %collective-permute-start = (f32[8,1280]{1,0:T(8,128)}, f32[8,1280]{1,0:T(8,128)S(1)}, u32[]{:S(2)}, u32[]{:S(2)}) collective-permute-start(f32[8,1280]{1,0:T(8,128)} %get-tuple-element.19.down_ref), channel_id=1, source_target_pairs={{0,1},{1,2},{2,3},{3,0},{4,5},{5,6},{6,7},{7,4},{8,9},{9,10},{10,1... | collective-permute-start | bytes 122888 | tf_op jit(solution)/shard_map/ppermute | solution.py:587
  2.6 2.0 %collective-permute-start.1 = (f32[8,1280]{1,0:T(8,128)}, f32[8,1280]{1,0:T(8,128)S(1)}, u32[]{:S(2)}, u32[]{:S(2)}) collective-permute-start(f32[8,1280]{1,0:T(8,128)} %get-tuple-element.20.up_ref), channel_id=1, source_target_pairs={{0,3},{1,0},{2,1},{3,2},{4,7},{5,4},{6,5},{7,6},{8,11},{9,8},{10,9... | collective-permute-start | bytes 122888 | tf_op jit(solution)/shard_map/ppermute | solution.py:587
  4.6 2.2 %collective-permute-start.2 = (f32[8,512]{1,0:T(8,128)}, f32[8,512]{1,0:T(8,128)S(1)}, u32[]{:S(2)}, u32[]{:S(2)}) collective-permute-start(f32[8,512]{1,0:T(8,128)} %get-tuple-element.21.points_ref), channel_id=1, source_target_pairs={{0,2},{1,3},{2,0},{3,1},{4,6},{5,7},{6,4},{7,5},{8,10},{9,11},{10,... | collective-permute-start | bytes 49160 | tf_op jit(solution)/shard_map/ppermute | solution.py:587
  6.8 2.4 %collective-permute-done.2.far_ref = f32[8,512]{1,0:T(8,128)S(1)} collective-permute-done((f32[8,512]{1,0:T(8,128)}, f32[8,512]{1,0:T(8,128)S(1)}, u32[]{:S(2)}, u32[]{:S(2)}) %collective-permute-start.2) | collective-permute-done | bytes 16416 | tf_op jit(solution)/shard_map/ppermute | solution.py:587
  9.2 0.0 collective-permute-done.above_ref
  9.2 0.0 collective-permute-done.1.below_ref
  9.2 0.6 %copy-done.3 = f32[8,512]{1,0:T(8,128)} copy-done((f32[8,512]{1,0:T(8,128)}, f32[8,512]{1,0:T(8,128)S(1)}, u32[]{:S(2)}) %copy-start.3) | copy-done | bytes 16408
  9.8 0.0 copy-done.1
  9.8 0.0 copy-done.2
  9.8 1.7 %shard_map.101 = f32[8,8,640]{2,1,0:T(8,128)} custom-call(f32[8,2048]{1,0:T(8,128)} %get-tuple-element.18.partial_ref, bf16[8,2048]{1,0:T(8,128)(2,1)} %row_ref.3, bf16[8,2048]{1,0:T(8,128)(2,1)} %col_ref.3, bf16[8,2048]{1,0:T(8,128)(2,1)} %diff_ref.3, f32[8,1280]{1,0:T(8,128)} %get-tuple-element.19.down_ref, f32[8,1280]{1,0:T(8,128)} %get-tuple-element.20.up_ref, ...), custom_call_target="tpu_custom_call" | custom-call | tf_op jit(solution)/shard_map/pallas_call | solution.py:545
  11.5 5.9 %all-to-all-start = ((f32[8,8,640]{2,1,0:T(8,128)}), f32[8,8,640]{2,1,0:T(8,128)S(1)}, u32[]{:S(2)}, u32[]{:S(2)}) async-start(f32[8,8,640]{2,1,0:T(8,128)} %shard_map.101), calls=%async_computation | async-start | bytes 327680 | tf_op jit(solution)/shard_map/all_to_all | solution.py:604
  17.5 1.6 %shard_map.102 = (bf16[2,128,512]{2,1,0:T(8,128)(2,1)}, bf16[2,128,128]{2,1,0:T(8,128)(2,1)}, f32[8,128]{1,0:T(8,128)}) custom-call(f32[8,128]{1,0:T(8,128)} %get-tuple-element.22.sorted_ref), custom_call_target="tpu_custom_call" | custom-call | flops 655360 | bytes 524288 | tf_op jit(solution)/shard_map/pallas_call | solution.py:545
  19.1 5.9 %all-to-all-done.x_ref = f32[8,8,640]{2,1,0:T(8,128)S(1)} async-done(((f32[8,8,640]{2,1,0:T(8,128)}), f32[8,8,640]{2,1,0:T(8,128)S(1)}, u32[]{:S(2)}, u32[]{:S(2)}) %all-to-all-start) | async-done | bytes 163872 | tf_op jit(solution)/shard_map/all_to_all | solution.py:604
  25.0 0.7 %copy-done = f32[8,8,640]{2,1,0:T(8,128)} copy-done((f32[8,8,640]{2,1,0:T(8,128)}, f32[8,8,640]{2,1,0:T(8,128)S(1)}, u32[]{:S(2)}) %copy-start) | copy-done | bytes 163864
  25.7 2.6 %shard_map.103 = (f32[8,512]{1,0:T(8,128)}, f32[8,512]{1,0:T(8,128)}, f32[8,512]{1,0:T(8,128)}, f32[8,512]{1,0:T(8,128)}) custom-call(f32[8,8,640]{2,1,0:T(8,128)} %copy-done, f32[8,128]{1,0:T(8,128)} %get-tuple-element.22.sorted_ref, f32[8,128]{1,0:T(8,128)} %get-tuple-element.23.noise_ref, bf16[2,128,512]{2,1,0:T(8,128)(2,1)} %get-tuple-element.24.columns_ref, ...), custom_call_target="tpu_custom_call" | custom-call | tf_op jit(solution)/shard_map/pallas_call | solution.py:545
  28.3 0.3 collective-permute-start.3
  28.6 1.0 %collective-permute-start.4 = (f32[8,512]{1,0:T(8,128)}, f32[8,512]{1,0:T(8,128)S(1)}, u32[]{:S(2)}, u32[]{:S(2)}) collective-permute-start(f32[8,512]{1,0:T(8,128)} %get-tuple-element.29), channel_id=1, source_target_pairs={{0,8},{4,12},{8,0},{12,4},{16,24},{20,28},{24,16},{28,20},{1,9},{5... | collective-permute-start | bytes 49160 | tf_op jit(solution)/shard_map/ppermute | solution.py:612
  29.6 2.1 %collective-permute-start.5 = (f32[8,512]{1,0:T(8,128)}, f32[8,512]{1,0:T(8,128)S(1)}, u32[]{:S(2)}, u32[]{:S(2)}) collective-permute-start(f32[8,512]{1,0:T(8,128)} %get-tuple-element.30), channel_id=1, source_target_pairs={{0,12},{4,8},{8,4},{12,0},{16,28},{20,24},{24,20},{28,16},{1,13},{... | collective-permute-start | bytes 49160 | tf_op jit(solution)/shard_map/ppermute | solution.py:612
  31.8 0.5 %collective-permute-done.3.refs_1_ = f32[8,512]{1,0:T(8,128)S(1)} collective-permute-done((f32[8,512]{1,0:T(8,128)}, f32[8,512]{1,0:T(8,128)S(1)}, u32[]{:S(2)}, u32[]{:S(2)}) %collective-permute-start.3) | collective-permute-done | bytes 16416 | tf_op jit(solution)/shard_map/ppermute | solution.py:612
  32.2 0.3 collective-permute-done.4.refs_2_
  32.5 1.9 %collective-permute-done.5.refs_3_ = f32[8,512]{1,0:T(8,128)S(1)} collective-permute-done((f32[8,512]{1,0:T(8,128)}, f32[8,512]{1,0:T(8,128)S(1)}, u32[]{:S(2)}, u32[]{:S(2)}) %collective-permute-start.5) | collective-permute-done | bytes 16416 | tf_op jit(solution)/shard_map/ppermute | solution.py:612
  34.5 0.6 %copy-done.6 = f32[8,512]{1,0:T(8,128)} copy-done((f32[8,512]{1,0:T(8,128)}, f32[8,512]{1,0:T(8,128)S(1)}, u32[]{:S(2)}) %copy-start.6) | copy-done | bytes 16408
  35.1 1.4 %shard_map.104 = f32[1,8,2048]{2,1,0:T(8,128)} custom-call(f32[8,512]{1,0:T(8,128)} %get-tuple-element.27.refs_0_, f32[8,512]{1,0:T(8,128)} %copy-done.4, f32[8,512]{1,0:T(8,128)} %copy-done.5, f32[8,512]{1,0:T(8,128)} %copy-done.6), custom_call_target="tpu_custom_call" | custom-call | tf_op jit(solution)/shard_map/pallas_call | solution.py:545
  (9 shorter events, 0.0 us)
Async XLA Ops:
  2.0 7.1 %collective-permute-start = (f32[8,1280]{1,0:T(8,128)}, f32[8,1280]{1,0:T(8,128)S(1)}, u32[]{:S(2)}, u32[]{:S(2)}) collective-permute-start(f32[8,1280]{1,0:T(8,128)} %get-tuple-element.19.down_ref), channel_id=1, source_target_pairs={{0,1},{1,2},{2,3},{3,0},{4,5},{5,6},{6,7},{7,4},{8,9},{9,10},{10,1... | collective-permute-start | bytes 122888 | tf_op jit(solution)/shard_map/ppermute | solution.py:587
  2.6 6.6 %collective-permute-start.1 = (f32[8,1280]{1,0:T(8,128)}, f32[8,1280]{1,0:T(8,128)S(1)}, u32[]{:S(2)}, u32[]{:S(2)}) collective-permute-start(f32[8,1280]{1,0:T(8,128)} %get-tuple-element.20.up_ref), channel_id=1, source_target_pairs={{0,3},{1,0},{2,1},{3,2},{4,7},{5,4},{6,5},{7,6},{8,11},{9,8},{10,9... | collective-permute-start | bytes 122888 | tf_op jit(solution)/shard_map/ppermute | solution.py:587
  4.6 4.6 %collective-permute-start.2 = (f32[8,512]{1,0:T(8,128)}, f32[8,512]{1,0:T(8,128)S(1)}, u32[]{:S(2)}, u32[]{:S(2)}) collective-permute-start(f32[8,512]{1,0:T(8,128)} %get-tuple-element.21.points_ref), channel_id=1, source_target_pairs={{0,2},{1,3},{2,0},{3,1},{4,6},{5,7},{6,4},{7,5},{8,10},{9,11},{10,... | collective-permute-start | bytes 49160 | tf_op jit(solution)/shard_map/ppermute | solution.py:587
  9.2 0.6 %copy-start.3 = (f32[8,512]{1,0:T(8,128)}, f32[8,512]{1,0:T(8,128)S(1)}, u32[]{:S(2)}) copy-start(f32[8,512]{1,0:T(8,128)S(1)} %collective-permute-done.2.far_ref) | copy-start | bytes 49156
  9.2 0.6 %copy-start.1 = (f32[8,1280]{1,0:T(8,128)}, f32[8,1280]{1,0:T(8,128)S(1)}, u32[]{:S(2)}) copy-start(f32[8,1280]{1,0:T(8,128)S(1)} %collective-permute-done.above_ref) | copy-start | bytes 122884
  9.2 0.6 %copy-start.2 = (f32[8,1280]{1,0:T(8,128)}, f32[8,1280]{1,0:T(8,128)S(1)}, u32[]{:S(2)}) copy-start(f32[8,1280]{1,0:T(8,128)S(1)} %collective-permute-done.1.below_ref) | copy-start | bytes 122884
  11.5 13.5 %all-to-all-start = ((f32[8,8,640]{2,1,0:T(8,128)}), f32[8,8,640]{2,1,0:T(8,128)S(1)}, u32[]{:S(2)}, u32[]{:S(2)}) async-start(f32[8,8,640]{2,1,0:T(8,128)} %shard_map.101), calls=%async_computation | async-start | bytes 327680 | tf_op jit(solution)/shard_map/all_to_all | solution.py:604
  25.0 0.7 %copy-start = (f32[8,8,640]{2,1,0:T(8,128)}, f32[8,8,640]{2,1,0:T(8,128)S(1)}, u32[]{:S(2)}) copy-start(f32[8,8,640]{2,1,0:T(8,128)S(1)} %all-to-all-done.x_ref) | copy-start | bytes 491524
  28.3 3.9 %collective-permute-start.3 = (f32[8,512]{1,0:T(8,128)}, f32[8,512]{1,0:T(8,128)S(1)}, u32[]{:S(2)}, u32[]{:S(2)}) collective-permute-start(f32[8,512]{1,0:T(8,128)} %get-tuple-element.28), channel_id=1, source_target_pairs={{0,4},{4,0},{8,12},{12,8},{16,20},{20,16},{24,28},{28,24},{1,5},{5... | collective-permute-start | bytes 49160 | tf_op jit(solution)/shard_map/ppermute | solution.py:612
  28.6 3.9 %collective-permute-start.4 = (f32[8,512]{1,0:T(8,128)}, f32[8,512]{1,0:T(8,128)S(1)}, u32[]{:S(2)}, u32[]{:S(2)}) collective-permute-start(f32[8,512]{1,0:T(8,128)} %get-tuple-element.29), channel_id=1, source_target_pairs={{0,8},{4,12},{8,0},{12,4},{16,24},{20,28},{24,16},{28,20},{1,9},{5... | collective-permute-start | bytes 49160 | tf_op jit(solution)/shard_map/ppermute | solution.py:612
  29.6 4.8 %collective-permute-start.5 = (f32[8,512]{1,0:T(8,128)}, f32[8,512]{1,0:T(8,128)S(1)}, u32[]{:S(2)}, u32[]{:S(2)}) collective-permute-start(f32[8,512]{1,0:T(8,128)} %get-tuple-element.30), channel_id=1, source_target_pairs={{0,12},{4,8},{8,4},{12,0},{16,28},{20,24},{24,20},{28,16},{1,13},{... | collective-permute-start | bytes 49160 | tf_op jit(solution)/shard_map/ppermute | solution.py:612
  32.2 2.3 %copy-start.4 = (f32[8,512]{1,0:T(8,128)}, f32[8,512]{1,0:T(8,128)S(1)}, u32[]{:S(2)}) copy-start(f32[8,512]{1,0:T(8,128)S(1)} %collective-permute-done.3.refs_1_) | copy-start | bytes 49156
  32.5 1.9 %copy-start.5 = (f32[8,512]{1,0:T(8,128)}, f32[8,512]{1,0:T(8,128)S(1)}, u32[]{:S(2)}) copy-start(f32[8,512]{1,0:T(8,128)S(1)} %collective-permute-done.4.refs_2_) | copy-start | bytes 49156
  34.5 0.6 %copy-start.6 = (f32[8,512]{1,0:T(8,128)}, f32[8,512]{1,0:T(8,128)S(1)}, u32[]{:S(2)}) copy-start(f32[8,512]{1,0:T(8,128)S(1)} %collective-permute-done.5.refs_3_) | copy-start | bytes 49156

commit v2 on v1

--- a/solution.py
+++ b/solution.py
@@ -164,6 +164,7 @@
 CROSS = [(0, 0), (-1, 0), (1, 0), (0, -1), (0, 1)]
 TILES = -(-(len(POINTS) + 3 * len(CROSS)) // SUBLANES)
 PARTS = 4
+VMEM_GRANT = 8 << 20
 
 
 def iota(axis, shape=(SUBLANES, LANES)):
@@ -192,23 +193,54 @@
 
 def start_kernel(
     sizes,
-    q_ref,
+    q_hbm,
+    row_hbm,
+    col_hbm,
+    diff_hbm,
+    owner_hbm,
+    cell_hbm,
+    order_hbm,
+    value_hbm,
+    variance_hbm,
+    noise_hbm,
+    down_ref,
+    up_ref,
+    points_ref,
+    partial_ref,
+    sorted_ref,
+    noise_out,
     row_ref,
     col_ref,
     diff_ref,
+    q_ref,
     owner_ref,
     cell_ref,
     order_ref,
     value_ref,
     variance_ref,
     noise_ref,
-    down_ref,
-    up_ref,
-    points_ref,
-    partial_ref,
-    sorted_ref,
-    noise_out,
+    arrived,
 ):
+    fetched = (
+        (owner_hbm, owner_ref),
+        (cell_hbm, cell_ref),
+        (order_hbm, order_ref),
+        (value_hbm, value_ref),
+        (variance_hbm, variance_ref),
+        (noise_hbm, noise_ref),
+        (q_hbm, q_ref),
+        (row_hbm, row_ref),
+        (col_hbm, col_ref),
+        (diff_hbm, diff_ref),
+    )
+    copies = [
+        pltpu.make_async_copy(source, target, arrived.at[n])
+        for n, (source, target) in enumerate(fetched)
+    ]
+    for copy in copies:
+        copy.start()
+    for copy in copies[:6]:
+        copy.wait()
     reg_count, region_rows, slab_rows, columns = sizes
     grid_rows = reg_count * region_rows
     packed = columns // SUBLANES
@@ -246,6 +278,8 @@
     orow = row_of(table, 0).astype(jnp.int32)
     ocol = row_of(table, 1).astype(jnp.int32)
 
+    for copy in copies[6:]:
+        copy.wait()
     q = q_ref[0]
     rates = [r[...].astype(jnp.float32) for r in (row_ref, col_ref, diff_ref)]
     local_row = orow - me * region_rows
@@ -540,15 +574,16 @@
         out_ref[0, :, pl.ds(pl.multiple_of(part * width, LANES), width)] = ref[...]
 
 
-def call(kernel, outs, args, scratch=(), cost=None):
-    space = pl.BlockSpec(memory_space=pltpu.VMEM)
+def call(kernel, outs, args, scratch=(), cost=None, space=pltpu.VMEM):
+    held = pl.BlockSpec(memory_space=pltpu.VMEM)
     return pl.pallas_call(
         kernel,
         out_shape=[jax.ShapeDtypeStruct(s, d) for s, d in outs],
-        in_specs=[space] * len(args),
-        out_specs=[space] * len(outs),
+        in_specs=[pl.BlockSpec(memory_space=space)] * len(args),
+        out_specs=[held] * len(outs),
         scratch_shapes=list(scratch),
         cost_estimate=cost,
+        compiler_params=pltpu.CompilerParams(vmem_limit_bytes=VMEM_GRANT),
     )(*args)
 
 
@@ -577,10 +612,16 @@
     message = (SUBLANES, 3 * packed + TILES * LANES)
     rates = (courant_row, courant_column, diffusion)
     flat = [x.reshape(1, LANES) for x in (obs_owner, obs_cell, obs_order, obs_value, observation_variance)]
-    down, up, points, partial, table, noise = call(
+    operands = (prior_tracer_draws, *rates, *flat, obs_noise.T)
+    down, up, points, partial, table, noise, *rates = call(
         functools.partial(start_kernel, sizes),
-        [(message, f32), (message, f32), (points_shape, f32), (field, f32), (tile, f32), (tile, f32)],
-        (prior_tracer_draws, *rates, *flat, obs_noise.T),
+        [(message, f32), (message, f32), (points_shape, f32), (field, f32), (tile, f32), (tile, f32)]
+        + [(x.shape, x.dtype) for x in rates],
+        [pltpu.with_memory_space_constraint(x, pltpu.HBM) for x in operands],
+        scratch=[pltpu.VMEM(prior_tracer_draws.shape, f32)]
+        + [pltpu.VMEM(x.shape, x.dtype) for x in operands[4:]]
+        + [pltpu.SemaphoreType.DMA((len(operands),))],
+        space=pltpu.HBM,
     )
 
     def shifted(x, by):

time: 36.9 us -> 30.5 us (0.83)
  Pallas kernels: 9.38 us -> 3.95 us
  local copies, waits for them, and re-layouts: 1.87 us -> 0 us
  waiting for transfers between devices: 11 us -> 12 us
    pallas_call x5, Pallas kernels: 9.38 us -> 3.95 us  [call(): pl.pallas_call(kernel, out_shape=[jax.ShapeDtypeStruct(s, d) for s, d in...]
    unnamed x14 -> x0, local copies, waits for them, and re-layouts: 1.87 us -> none
    all_to_all x1, waiting for transfers between devices: 5.94 us -> 7.32 us  [on_tile(): slabs = lax.all_to_all(send, 'mem', split_axis=0, concat_axis=0, tiled=True)]
  transfers between devices with their start and end apart: 7 -> 7, of which waited for: 5 -> 5; matrix products, arithmetic and copies ran while one was open for 0% -> 0% of each run, Pallas kernels for 4% -> 1%
where the time goes in v2:
time: 30.5 us; the launch traced here: 30.2 us
  starting transfers between devices  14.2 us (47%)
  waiting for transfers between devices  12 us (39%)
  Pallas kernels  3.95 us (13%)
    all_to_all x1, waiting for transfers between devices, on_tile(): slabs = lax.all_to_all(send, 'mem', split_axis=0, concat_axis=0, tiled=True)  7.32 us
    all_to_all x1, starting transfers between devices, on_tile(): slabs = lax.all_to_all(send, 'mem', split_axis=0, concat_axis=0, tiled=True)  5.93 us
    ppermute x3, starting transfers between devices, shifted(): lax.ppermute(x, 'reg', [(i, (i + by) % reg_count) for i in range(reg_coun...  4.76 us
    pallas_call x5, Pallas kernels, call(): pl.pallas_call(kernel, out_shape=[jax.ShapeDtypeStruct(s, d) for s, d in...  3.95 us
    ppermute x3, starting transfers between devices, on_tile(): lax.ppermute(pieces[x], 'mem', [(i, i ^ x) for i in range(mem_count)])  3.55 us
    ppermute x3, waiting for transfers between devices, on_tile(): lax.ppermute(pieces[x], 'mem', [(i, i ^ x) for i in range(mem_count)])  2.5 us
    ppermute x3, waiting for transfers between devices, shifted(): lax.ppermute(x, 'reg', [(i, (i + by) % reg_count) for i in range(reg_coun...  2.16 us
  transfers between devices with their start and end apart: 7, of which 5 were waited for; matrix products, arithmetic and copies ran while one was open for 0% of the time, Pallas kernels for 1%

profile of v2, /device:TPU:0, one launch (start us, length us, event | category | flops | bytes accessed | tf_op | source)
XLA Modules:
  0.0 30.2 jit_solution(2645304219966635983)
XLA Ops:
  0.0 1.3 %shard_map.100 = (f32[8,1280]{1,0:T(8,128)S(1)}, f32[8,1280]{1,0:T(8,128)S(1)}, f32[8,512]{1,0:T(8,128)S(1)}, f32[8,2048]{1,0:T(8,128)S(1)}, f32[8,128]{1,0:T(8,...) custom-call(f32[1,8,2048]{2,1,0:T(8,128)} %q_hbm.1, ...), custom_call_target="tpu_custom_call" | custom-call | tf_op jit(solution)/shard_map/pallas_call | solution.py:579
  1.3 0.5 %collective-permute-start = (f32[8,1280]{1,0:T(8,128)S(1)}, f32[8,1280]{1,0:T(8,128)S(1)}, u32[]{:S(2)}, u32[]{:S(2)}) collective-permute-start(f32[8,1280]{1,0:T(8,128)S(1)} %get-tuple-element.25.down_ref), channel_id=1, source_target_pairs={{0,1},{1,2},{2,3},{3,0},{4,5},{5,6},{6,7},{7,4},{8,9},{9,10},{10,1... | collective-permute-start | bytes 122888 | tf_op jit(solution)/shard_map/ppermute | solution.py:628
  1.9 2.0 %collective-permute-start.1 = (f32[8,1280]{1,0:T(8,128)S(1)}, f32[8,1280]{1,0:T(8,128)S(1)}, u32[]{:S(2)}, u32[]{:S(2)}) collective-permute-start(f32[8,1280]{1,0:T(8,128)S(1)} %get-tuple-element.26.up_ref), channel_id=1, source_target_pairs={{0,3},{1,0},{2,1},{3,2},{4,7},{5,4},{6,5},{7,6},{8,11},{9,8},{10,9... | collective-permute-start | bytes 122888 | tf_op jit(solution)/shard_map/ppermute | solution.py:628
  3.9 2.2 %collective-permute-start.2 = (f32[8,512]{1,0:T(8,128)S(1)}, f32[8,512]{1,0:T(8,128)S(1)}, u32[]{:S(2)}, u32[]{:S(2)}) collective-permute-start(f32[8,512]{1,0:T(8,128)S(1)} %get-tuple-element.27.points_ref), channel_id=1, source_target_pairs={{0,2},{1,3},{2,0},{3,1},{4,6},{5,7},{6,4},{7,5},{8,10},{9,11},{10,... | collective-permute-start | bytes 49160 | tf_op jit(solution)/shard_map/ppermute | solution.py:628
  6.1 2.2 %collective-permute-done.2.far_ref = f32[8,512]{1,0:T(8,128)S(1)} collective-permute-done((f32[8,512]{1,0:T(8,128)S(1)}, f32[8,512]{1,0:T(8,128)S(1)}, u32[]{:S(2)}, u32[]{:S(2)}) %collective-permute-start.2) | collective-permute-done | bytes 16416 | tf_op jit(solution)/shard_map/ppermute | solution.py:628
  8.3 0.0 collective-permute-done.above_ref
  8.3 0.0 collective-permute-done.1.below_ref
  8.3 0.8 %shard_map.101 = f32[8,8,640]{2,1,0:T(8,128)} custom-call(f32[8,2048]{1,0:T(8,128)S(1)} %get-tuple-element.21.partial_ref, bf16[8,2048]{1,0:T(8,128)(2,1)S(1)} %get-tuple-element.22.row_ref, bf16[8,2048]{1,0:T(8,128)(2,1)S(1)} %get-tuple-element.23.col_ref, bf16[8,2048]{1,0:T(8,128)(2,1)S(1)} %get-tuple-element.24.diff_ref, ...), custom_call_target="tpu_custom_call" | custom-call | tf_op jit(solution)/shard_map/pallas_call | solution.py:579
  9.1 5.9 %all-to-all-start = ((f32[8,8,640]{2,1,0:T(8,128)}), f32[8,8,640]{2,1,0:T(8,128)S(1)}, u32[]{:S(2)}, u32[]{:S(2)}) async-start(f32[8,8,640]{2,1,0:T(8,128)} %shard_map.101), calls=%async_computation | async-start | bytes 327680 | tf_op jit(solution)/shard_map/all_to_all | solution.py:645
  15.0 0.2 shard_map.102
  15.2 7.3 %all-to-all-done.x_ref = f32[8,8,640]{2,1,0:T(8,128)S(1)} async-done(((f32[8,8,640]{2,1,0:T(8,128)}), f32[8,8,640]{2,1,0:T(8,128)S(1)}, u32[]{:S(2)}, u32[]{:S(2)}) %all-to-all-start) | async-done | bytes 163872 | tf_op jit(solution)/shard_map/all_to_all | solution.py:645
  22.6 0.9 %shard_map.103 = (f32[8,512]{1,0:T(8,128)S(1)}, f32[8,512]{1,0:T(8,128)S(1)}, f32[8,512]{1,0:T(8,128)S(1)}, f32[8,512]{1,0:T(8,128)S(1)}) custom-call(f32[8,8,640]{2,1,0:T(8,128)S(1)} %all-to-all-done.x_ref, f32[8,128]{1,0:T(8,128)S(1)} %get-tuple-element.28.sorted_ref, f32[8,128]{1,0:T(8,128)S(1)} %get-tuple-element.29.noise_ref, ...), custom_call_target="tpu_custom_call" | custom-call | tf_op jit(solution)/shard_map/pallas_call | solution.py:579
  23.5 0.4 %collective-permute-start.3 = (f32[8,512]{1,0:T(8,128)S(1)}, f32[8,512]{1,0:T(8,128)S(1)}, u32[]{:S(2)}, u32[]{:S(2)}) collective-permute-start(f32[8,512]{1,0:T(8,128)S(1)} %get-tuple-element.34), channel_id=1, source_target_pairs={{0,4},{4,0},{8,12},{12,8},{16,20},{20,16},{24,28},{28,24},{1,5},{5... | collective-permute-start | bytes 49160 | tf_op jit(solution)/shard_map/ppermute | solution.py:653
  23.9 1.0 %collective-permute-start.4 = (f32[8,512]{1,0:T(8,128)S(1)}, f32[8,512]{1,0:T(8,128)S(1)}, u32[]{:S(2)}, u32[]{:S(2)}) collective-permute-start(f32[8,512]{1,0:T(8,128)S(1)} %get-tuple-element.35), channel_id=1, source_target_pairs={{0,8},{4,12},{8,0},{12,4},{16,24},{20,28},{24,16},{28,20},{1,9},{5... | collective-permute-start | bytes 49160 | tf_op jit(solution)/shard_map/ppermute | solution.py:653
  24.9 2.1 %collective-permute-start.5 = (f32[8,512]{1,0:T(8,128)S(1)}, f32[8,512]{1,0:T(8,128)S(1)}, u32[]{:S(2)}, u32[]{:S(2)}) collective-permute-start(f32[8,512]{1,0:T(8,128)S(1)} %get-tuple-element.36), channel_id=1, source_target_pairs={{0,12},{4,8},{8,4},{12,0},{16,28},{20,24},{24,20},{28,16},{1,13},{... | collective-permute-start | bytes 49160 | tf_op jit(solution)/shard_map/ppermute | solution.py:653
  27.1 0.2 collective-permute-done.3.refs_1_
  27.3 0.3 %collective-permute-done.4.refs_2_ = f32[8,512]{1,0:T(8,128)S(1)} collective-permute-done((f32[8,512]{1,0:T(8,128)S(1)}, f32[8,512]{1,0:T(8,128)S(1)}, u32[]{:S(2)}, u32[]{:S(2)}) %collective-permute-start.4) | collective-permute-done | bytes 16416 | tf_op jit(solution)/shard_map/ppermute | solution.py:653
  27.6 1.9 %collective-permute-done.5.refs_3_ = f32[8,512]{1,0:T(8,128)S(1)} collective-permute-done((f32[8,512]{1,0:T(8,128)S(1)}, f32[8,512]{1,0:T(8,128)S(1)}, u32[]{:S(2)}, u32[]{:S(2)}) %collective-permute-start.5) | collective-permute-done | bytes 16416 | tf_op jit(solution)/shard_map/ppermute | solution.py:653
  29.6 0.6 %shard_map.104 = f32[1,8,2048]{2,1,0:T(8,128)} custom-call(f32[8,512]{1,0:T(8,128)S(1)} %get-tuple-element.33.refs_0_, f32[8,512]{1,0:T(8,128)S(1)} %collective-permute-done.3.refs_1_, f32[8,512]{1,0:T(8,128)S(1)} %collective-permute-done.4.refs_2_, f32[8,512]{1,0:T(8,128)S(1)} %collective-permute-done.5.refs_3_), custom_call_target="tpu_custom_call" | custom-call | tf_op jit(solution)/shard_map/pallas_call | solution.py:579
Async XLA Ops:
  1.3 6.9 %collective-permute-start = (f32[8,1280]{1,0:T(8,128)S(1)}, f32[8,1280]{1,0:T(8,128)S(1)}, u32[]{:S(2)}, u32[]{:S(2)}) collective-permute-start(f32[8,1280]{1,0:T(8,128)S(1)} %get-tuple-element.25.down_ref), channel_id=1, source_target_pairs={{0,1},{1,2},{2,3},{3,0},{4,5},{5,6},{6,7},{7,4},{8,9},{9,10},{10,1... | collective-permute-start | bytes 122888 | tf_op jit(solution)/shard_map/ppermute | solution.py:628
  1.9 6.4 %collective-permute-start.1 = (f32[8,1280]{1,0:T(8,128)S(1)}, f32[8,1280]{1,0:T(8,128)S(1)}, u32[]{:S(2)}, u32[]{:S(2)}) collective-permute-start(f32[8,1280]{1,0:T(8,128)S(1)} %get-tuple-element.26.up_ref), channel_id=1, source_target_pairs={{0,3},{1,0},{2,1},{3,2},{4,7},{5,4},{6,5},{7,6},{8,11},{9,8},{10,9... | collective-permute-start | bytes 122888 | tf_op jit(solution)/shard_map/ppermute | solution.py:628
  3.9 4.4 %collective-permute-start.2 = (f32[8,512]{1,0:T(8,128)S(1)}, f32[8,512]{1,0:T(8,128)S(1)}, u32[]{:S(2)}, u32[]{:S(2)}) collective-permute-start(f32[8,512]{1,0:T(8,128)S(1)} %get-tuple-element.27.points_ref), channel_id=1, source_target_pairs={{0,2},{1,3},{2,0},{3,1},{4,6},{5,7},{6,4},{7,5},{8,10},{9,11},{10,... | collective-permute-start | bytes 49160 | tf_op jit(solution)/shard_map/ppermute | solution.py:628
  9.1 13.5 %all-to-all-start = ((f32[8,8,640]{2,1,0:T(8,128)}), f32[8,8,640]{2,1,0:T(8,128)S(1)}, u32[]{:S(2)}, u32[]{:S(2)}) async-start(f32[8,8,640]{2,1,0:T(8,128)} %shard_map.101), calls=%async_computation | async-start | bytes 327680 | tf_op jit(solution)/shard_map/all_to_all | solution.py:645
  23.5 3.8 %collective-permute-start.3 = (f32[8,512]{1,0:T(8,128)S(1)}, f32[8,512]{1,0:T(8,128)S(1)}, u32[]{:S(2)}, u32[]{:S(2)}) collective-permute-start(f32[8,512]{1,0:T(8,128)S(1)} %get-tuple-element.34), channel_id=1, source_target_pairs={{0,4},{4,0},{8,12},{12,8},{16,20},{20,16},{24,28},{28,24},{1,5},{5... | collective-permute-start | bytes 49160 | tf_op jit(solution)/shard_map/ppermute | solution.py:653
  23.9 3.7 %collective-permute-start.4 = (f32[8,512]{1,0:T(8,128)S(1)}, f32[8,512]{1,0:T(8,128)S(1)}, u32[]{:S(2)}, u32[]{:S(2)}) collective-permute-start(f32[8,512]{1,0:T(8,128)S(1)} %get-tuple-element.35), channel_id=1, source_target_pairs={{0,8},{4,12},{8,0},{12,4},{16,24},{20,28},{24,16},{28,20},{1,9},{5... | collective-permute-start | bytes 49160 | tf_op jit(solution)/shard_map/ppermute | solution.py:653
  24.9 4.6 %collective-permute-start.5 = (f32[8,512]{1,0:T(8,128)S(1)}, f32[8,512]{1,0:T(8,128)S(1)}, u32[]{:S(2)}, u32[]{:S(2)}) collective-permute-start(f32[8,512]{1,0:T(8,128)S(1)} %get-tuple-element.36), channel_id=1, source_target_pairs={{0,12},{4,8},{8,4},{12,0},{16,28},{20,24},{24,20},{28,16},{1,13},{... | collective-permute-start | bytes 49160 | tf_op jit(solution)/shard_map/ppermute | solution.py:653

commit v3 on v2

--- a/solution.py
+++ b/solution.py
@@ -163,7 +163,11 @@
 POINTS = [(dr, dc) for dr in range(-2, 3) for dc in range(-2, 3) if abs(dr) + abs(dc) <= 2]
 CROSS = [(0, 0), (-1, 0), (1, 0), (0, -1), (0, 1)]
 TILES = -(-(len(POINTS) + 3 * len(CROSS)) // SUBLANES)
-PARTS = 4
+CHUNK = 4 * LANES
+CODE_STEP = 2.0**-20
+CODE_TOP = 32767.0
+SEEN_UNIT = 2.0**-11
+SEEN_REST = 2.0**-15
 VMEM_GRANT = 8 << 20
 
 
@@ -342,18 +346,16 @@
 
 def taper_kernel(sizes, sorted_ref, columns_ref, obs_ref, rows_ref):
     reg_count, region_rows, slab_rows, columns = sizes
-    width = columns // PARTS
     grid_rows = reg_count * region_rows
     row_scale, col_scale = float(region_rows // 2), float(columns // 4)
-    part = lax.axis_index("mem") % PARTS
     me = lax.axis_index("reg")
     square = (LANES, LANES)
     row_lanes = jnp.broadcast_to(sorted_ref[0:1, :], square)
     col_lanes = jnp.broadcast_to(sorted_ref[1:2, :], square)
     row_subs = row_lanes.T
     col_subs = col_lanes.T
-    for t in range(width // LANES):
-        at = (part * width + t * LANES + iota(1, square)).astype(jnp.float32)
+    for t in range(columns // LANES):
+        at = (t * LANES + iota(1, square)).astype(jnp.float32)
         high, low = halves(bell_of(at - col_subs, float(columns), col_scale))
         columns_ref[0, :, t * LANES : (t + 1) * LANES] = high
         columns_ref[1, :, t * LANES : (t + 1) * LANES] = low
@@ -379,12 +381,12 @@
     above_ref,
     below_ref,
     far_ref,
+    field_ref,
     out_ref,
     edge_ref,
 ):
     reg_count, region_rows, slab_rows, columns = sizes
     packed = columns // SUBLANES
-    width = columns // PARTS
     wide = iota(0, (SUBLANES, columns))
     rate_row, rate_col, rate_diff = [
         r[...].astype(jnp.float32) for r in (row_ref, col_ref, diff_ref)
@@ -440,11 +442,20 @@
         )
 
     q1 = {p: at_point(q0, p) for p in CROSS}
-    seen = jnp.broadcast_to(at_point(q1, (0, 0)), (SUBLANES, LANES))
+    seen = jnp.broadcast_to(at_point(q1, (0, 0)), (SUBLANES, LANES)) / SEEN_UNIT
+    whole = jnp.round(seen)
+    rest = jnp.round((seen - whole) / SEEN_REST)
+    field_ref[...] = field
+    peak = jnp.max(jnp.max(jnp.abs(field), axis=1, keepdims=True), axis=0, keepdims=True)
+    steps = jnp.maximum(jnp.ceil(peak * (1.0 / (CODE_TOP * CODE_STEP))), 1.0)
+    code = jnp.round(field * (1.0 / (steps * CODE_STEP)))
+    sub = iota(0)
+    tail = jnp.where(
+        sub == 0, whole, jnp.where(sub == 1, rest, jnp.broadcast_to(steps, (SUBLANES, LANES)))
+    )
+    message = jnp.concatenate([code, tail], axis=1).astype(jnp.int32).astype(jnp.int16)
     for d in range(out_ref.shape[0]):
-        g = d % PARTS
-        out_ref[d, :, :width] = field[:, g * width : (g + 1) * width]
-        out_ref[d, :, width:] = seen
+        out_ref[d] = message
 
 
 def gain(anomaly, precision, innovation):
@@ -486,92 +497,110 @@
     return jnp.where(lane // half == block, x, pltpu.roll(x, half, axis=1))
 
 
-def weigh(rows, table_ref, block):
+def split(rows):
     half = LANES // 2
-    lane = iota(1, rows.shape)
     high = rows.astype(jnp.bfloat16).astype(jnp.float32)
-    left = jnp.where(lane < half, high, rows - high).astype(jnp.bfloat16)
-    high = table_ref[0, block * half : (block + 1) * half, :]
-    low = table_ref[1, block * half : (block + 1) * half, :]
-    return jnp.dot(
-        jnp.concatenate([left, left], axis=1),
-        jnp.concatenate([high, high, low, low], axis=0),
-        preferred_element_type=jnp.float32,
-    )
-
-
-def finish_kernel(sizes, x_ref, sorted_ref, noise_ref, columns_ref, obs_ref, rows_ref, *outs):
-    reg_count, region_rows, slab_rows, columns = sizes
+    left = jnp.where(iota(1, rows.shape) < half, high, rows - high).astype(jnp.bfloat16)
+    return jnp.concatenate([left, left], axis=1)
+
+
+def stacked(table_ref, block, part=slice(None)):
+    half = LANES // 2
+    high = table_ref[0, block * half : (block + 1) * half, part]
+    low = table_ref[1, block * half : (block + 1) * half, part]
+    return jnp.concatenate([high, high, low, low], axis=0)
+
+
+def finish_kernel(
+    sizes,
+    x_ref,
+    field_ref,
+    sorted_ref,
+    noise_ref,
+    columns_ref,
+    obs_ref,
+    rows_ref,
+    out_ref,
+    now_ref,
+):
+    columns = sizes[-1]
     members = x_ref.shape[0]
-    width = columns // PARTS
-    now_ref = outs[-1]
-    outs = outs[:-1]
     me = lax.axis_index("mem")
     sub, lane = iota(0), iota(1)
     half = LANES // 2
     seen = jnp.zeros((SUBLANES, LANES), jnp.float32)
+    steps = []
     for m in range(members):
-        seen = jnp.where(sub == m, x_ref[m, :, width:], seen)
+        tail = x_ref[m, :, columns:].astype(jnp.float32)
+        value = (row_of(tail, 0) + row_of(tail, 1) * SEEN_REST) * SEEN_UNIT
+        seen = jnp.where(sub == m, value, seen)
+        steps.append(row_of(tail, 2) * CODE_STEP)
     value, variance = row_of(sorted_ref, 2), row_of(sorted_ref, 3)
     observed = value + jnp.sqrt(variance) * noise_ref[...]
     inverse_variance = 1.0 / variance
     scale = 1.0 / (members - 1)
-    current = [x_ref[m, :, :width] for m in range(members)]
+    lefts = []
     for block in range(NBLK):
+        last = block + 1 == NBLK
         anomaly = seen - jnp.sum(seen, axis=0, keepdims=True) * (1.0 / members)
         precision = jnp.where(lane // half == block, inverse_variance, 0.0)
         gains = gain(anomaly, precision, observed - seen) * scale
         gains, local = twice(gains, block), twice(anomaly, block)
         pairs = [row_of(local, a) * gains for a in range(members)]
-        if block + 1 < NBLK:
-            moved = weigh(jnp.concatenate(pairs, axis=0), obs_ref, block)
+        row_taper = twice(rows_ref[...], block)
+        if last:
+            own = [
+                jnp.sum(jnp.where(sub == me, pair, 0.0), axis=0, keepdims=True) for pair in pairs
+            ]
+            lefts.append([row_taper * x for x in own])
+        else:
+            moved = jnp.dot(
+                split(jnp.concatenate(pairs, axis=0)),
+                stacked(obs_ref, block),
+                preferred_element_type=jnp.float32,
+            )
             for a in range(members):
                 seen = seen + row_of(anomaly, a) * moved[a * SUBLANES : (a + 1) * SUBLANES]
-        row_taper = twice(rows_ref[...], block)
-        mean = sum(current[1:], current[0]) * (1.0 / members)
-        centred = [x - mean for x in current]
-        if block + 1 < NBLK:
-            chosen = list(range(members))
-            terms = [
-                [row_taper * row_of(pairs[a], m) for m in chosen] for a in range(members)
-            ]
-            start = current
-        else:
-            for m in range(members):
-                now_ref[m] = current[m]
-            chosen = list(range(PARTS))
-            starts = [now_ref[me ^ x] for x in chosen]
-            terms = []
+            lefts.append([row_taper * row_of(pair, m) for pair in pairs for m in range(members)])
+    lefts = [split(jnp.concatenate(x, axis=0)) for x in lefts]
+
+    def added(starts, centred, weights):
+        updated = []
+        for n, total in enumerate(starts):
             for a in range(members):
-                held = pairs[a]
-                row = []
-                for x in chosen:
-                    mine = jnp.sum(jnp.where(sub == (me ^ x), held, 0.0), axis=0, keepdims=True)
-                    row.append(row_taper * mine)
-                terms.append(row)
-            start = starts
-        weights = weigh(
-            jnp.concatenate([t for row in terms for t in row], axis=0), columns_ref, block
-        )
-        updated = []
-        for n in range(len(chosen)):
-            total = start[n]
-            for a in range(members):
-                at = (a * len(chosen) + n) * SUBLANES
+                at = (a * len(starts) + n) * SUBLANES
                 total = total + centred[a] * weights[at : at + SUBLANES]
             updated.append(total)
-        current = updated
-    for ref, x in zip(outs, current):
-        ref[...] = x
-
-
-def join_kernel(columns, *refs):
-    out_ref = refs[-1]
-    width = columns // PARTS
-    me = lax.axis_index("mem")
-    for x, ref in enumerate(refs[:-1]):
-        part = (me ^ x) % PARTS
-        out_ref[0, :, pl.ds(pl.multiple_of(part * width, LANES), width)] = ref[...]
+        return updated
+
+    def centre(fields):
+        mean = sum(fields[1:], fields[0]) * (1.0 / members)
+        return [x - mean for x in fields]
+
+    for begin in range(0, columns, CHUNK):
+        part = slice(begin, begin + CHUNK)
+
+        def decoded(m, part=part):
+            return x_ref[m, :, part].astype(jnp.float32)
+
+        current = [decoded(m) * steps[m][:, :1] for m in range(members)]
+        for m in range(members):
+            now_ref[m] = current[m]
+        sent = now_ref[me]
+        for block in range(NBLK):
+            weights = jnp.dot(
+                lefts[block],
+                stacked(columns_ref, block, part),
+                preferred_element_type=jnp.float32,
+            )
+            if block + 1 < NBLK:
+                current = added(current, centre(current), weights)
+                for m in range(members):
+                    now_ref[m] = current[m]
+            else:
+                own = now_ref[me] + (field_ref[:, part] - sent)
+                (own,) = added([own], centre(current), weights)
+                out_ref[0, :, part] = own
 
 
 def call(kernel, outs, args, scratch=(), cost=None, space=pltpu.VMEM):
@@ -605,7 +634,6 @@
     mem_count, reg_count = lax.axis_size("mem"), lax.axis_size("reg")
     sizes = (reg_count, region_rows, region_rows // mem_count, columns)
     packed = columns // SUBLANES
-    width = columns // PARTS
     tile = (SUBLANES, LANES)
     field = (SUBLANES, columns)
     points_shape = (SUBLANES, TILES * LANES)
@@ -632,28 +660,22 @@
     far = [shifted(points, by) for by in range(2, reg_count - 1)]
     col_taper, obs_taper, row_taper = call(
         functools.partial(taper_kernel, sizes),
-        [((2, LANES, width), jnp.bfloat16), ((2, LANES, LANES), jnp.bfloat16), (tile, f32)],
+        [((2, LANES, columns), jnp.bfloat16), ((2, LANES, LANES), jnp.bfloat16), (tile, f32)],
         (table,),
-        cost=pl.CostEstimate(flops=10 * LANES * width, bytes_accessed=8 * LANES * width, transcendentals=LANES * width),
-    )
-    (send,) = call(
+        cost=pl.CostEstimate(flops=10 * LANES * columns, bytes_accessed=8 * LANES * columns, transcendentals=LANES * columns),
+    )
+    forecast, send = call(
         functools.partial(middle_kernel, sizes),
-        [((mem_count, SUBLANES, width + LANES), f32)],
+        [(field, f32), ((mem_count, SUBLANES, columns + LANES), jnp.int16)],
         (partial, *rates, down, up, points, above, below, sum(far[1:], far[0])),
         scratch=[pltpu.VMEM(field, f32)],
     )
     slabs = lax.all_to_all(send, "mem", split_axis=0, concat_axis=0, tiled=True)
-    pieces = call(
+    (out,) = call(
         functools.partial(finish_kernel, sizes),
-        [((SUBLANES, width), f32)] * PARTS,
-        (slabs, table, noise, col_taper, obs_taper, row_taper),
-        scratch=[pltpu.VMEM((members, SUBLANES, width), f32)],
-    )
-    back = [pieces[0]] + [
-        lax.ppermute(pieces[x], "mem", [(i, i ^ x) for i in range(mem_count)]) for x in range(1, PARTS)
-    ]
-    (out,) = call(
-        functools.partial(join_kernel, columns), [(prior_tracer_draws.shape, f32)], back
+        [(prior_tracer_draws.shape, f32)],
+        (slabs, forecast, table, noise, col_taper, obs_taper, row_taper),
+        scratch=[pltpu.VMEM((members, SUBLANES, CHUNK), f32)],
     )
     return out
 
@@ -666,8 +688,9 @@
         members == 1
         and noise[1] == counts[0] == region_rows == SUBLANES
         and noise[0] == NOB * NBLK == LANES
-        and counts[1] == PARTS
-        and columns % (PARTS * LANES) == 0
+        and counts[1] >= 4
+        and counts[1] & (counts[1] - 1) == 0
+        and columns % CHUNK == 0
         and columns & (columns - 1) == 0
     )
 

time: 30.5 us -> 26.5 us (0.87)
  starting transfers between devices: 14.2 us -> 10.7 us
  waiting for transfers between devices: 12 us -> 10.4 us
  Pallas kernels: 3.95 us -> 5.12 us
    ppermute x3 -> x0, starting transfers between devices: 3.55 us -> none  [on_tile(): lax.ppermute(pieces[x], 'mem', [(i, i ^ x) for i in range(mem_count)])]
    ppermute x3 -> x0, waiting for transfers between devices: 2.5 us -> none  [on_tile(): lax.ppermute(pieces[x], 'mem', [(i, i ^ x) for i in range(mem_count)])]
    pallas_call x5 -> x4, Pallas kernels: 3.95 us -> 5.12 us  [call(): pl.pallas_call(kernel, out_shape=[jax.ShapeDtypeStruct(s, d) for s, d in...]
    all_to_all x1, waiting for transfers between devices: 7.32 us -> 8.23 us  [on_tile(): slabs = lax.all_to_all(send, 'mem', split_axis=0, concat_axis=0, tiled=True)]
  transfers between devices with their start and end apart: 7 -> 4, of which waited for: 5 -> 2; matrix products, arithmetic and copies ran while one was open for 0% -> 0% of each run, Pallas kernels for 1% -> 3%
where the time goes in v3:
time: 26.5 us; the launch traced here: 26.2 us
  starting transfers between devices  10.7 us (40%)
  waiting for transfers between devices  10.4 us (39%)
  Pallas kernels  5.12 us (19%)
    all_to_all x1, waiting for transfers between devices, on_tile(): slabs = lax.all_to_all(send, 'mem', split_axis=0, concat_axis=0, tiled=True)  8.23 us
    all_to_all x1, starting transfers between devices, on_tile(): slabs = lax.all_to_all(send, 'mem', split_axis=0, concat_axis=0, tiled=True)  5.93 us
    pallas_call x4, Pallas kernels, call(): pl.pallas_call(kernel, out_shape=[jax.ShapeDtypeStruct(s, d) for s, d in...  5.12 us
    ppermute x3, starting transfers between devices, shifted(): lax.ppermute(x, 'reg', [(i, (i + by) % reg_count) for i in range(reg_coun...  4.76 us
    ppermute x3, waiting for transfers between devices, shifted(): lax.ppermute(x, 'reg', [(i, (i + by) % reg_count) for i in range(reg_coun...  2.16 us
  transfers between devices with their start and end apart: 4, of which 2 were waited for; matrix products, arithmetic and copies ran while one was open for 0% of the time, Pallas kernels for 3%

profile of v3, /device:TPU:0, one launch (start us, length us, event | category | flops | bytes accessed | tf_op | source)
XLA Modules:
  0.0 26.2 jit_solution(3405842003169216472)
XLA Ops:
  0.0 1.3 %shard_map.100 = (f32[8,1280]{1,0:T(8,128)S(1)}, f32[8,1280]{1,0:T(8,128)S(1)}, f32[8,512]{1,0:T(8,128)S(1)}, f32[8,2048]{1,0:T(8,128)S(1)}, f32[8,128]{1,0:T(8,...) custom-call(f32[1,8,2048]{2,1,0:T(8,128)} %q_hbm.1, ...), custom_call_target="tpu_custom_call" | custom-call | tf_op jit(solution)/shard_map/pallas_call | solution.py:608
  1.3 0.5 %collective-permute-start = (f32[8,1280]{1,0:T(8,128)S(1)}, f32[8,1280]{1,0:T(8,128)S(1)}, u32[]{:S(2)}, u32[]{:S(2)}) collective-permute-start(f32[8,1280]{1,0:T(8,128)S(1)} %get-tuple-element.23.down_ref), channel_id=1, source_target_pairs={{0,1},{1,2},{2,3},{3,0},{4,5},{5,6},{6,7},{7,4},{8,9},{9,10},{10,1... | collective-permute-start | bytes 122888 | tf_op jit(solution)/shard_map/ppermute | solution.py:656
  1.9 2.0 %collective-permute-start.1 = (f32[8,1280]{1,0:T(8,128)S(1)}, f32[8,1280]{1,0:T(8,128)S(1)}, u32[]{:S(2)}, u32[]{:S(2)}) collective-permute-start(f32[8,1280]{1,0:T(8,128)S(1)} %get-tuple-element.24.up_ref), channel_id=1, source_target_pairs={{0,3},{1,0},{2,1},{3,2},{4,7},{5,4},{6,5},{7,6},{8,11},{9,8},{10,9... | collective-permute-start | bytes 122888 | tf_op jit(solution)/shard_map/ppermute | solution.py:656
  3.9 2.2 %collective-permute-start.2 = (f32[8,512]{1,0:T(8,128)S(1)}, f32[8,512]{1,0:T(8,128)S(1)}, u32[]{:S(2)}, u32[]{:S(2)}) collective-permute-start(f32[8,512]{1,0:T(8,128)S(1)} %get-tuple-element.25.points_ref), channel_id=1, source_target_pairs={{0,2},{1,3},{2,0},{3,1},{4,6},{5,7},{6,4},{7,5},{8,10},{9,11},{10,... | collective-permute-start | bytes 49160 | tf_op jit(solution)/shard_map/ppermute | solution.py:656
  6.1 2.2 %collective-permute-done.2.far_ref = f32[8,512]{1,0:T(8,128)S(1)} collective-permute-done((f32[8,512]{1,0:T(8,128)S(1)}, f32[8,512]{1,0:T(8,128)S(1)}, u32[]{:S(2)}, u32[]{:S(2)}) %collective-permute-start.2) | collective-permute-done | bytes 16416 | tf_op jit(solution)/shard_map/ppermute | solution.py:656
  8.3 0.0 collective-permute-done.above_ref
  8.3 0.0 collective-permute-done.1.below_ref
  8.3 0.9 %shard_map.101 = (f32[8,2048]{1,0:T(8,128)S(1)}, s16[8,8,2176]{2,1,0:T(8,128)(2,1)}) custom-call(f32[8,2048]{1,0:T(8,128)S(1)} %get-tuple-element.19.partial_ref, bf16[8,2048]{1,0:T(8,128)(2,1)S(1)} %get-tuple-element.20.row_ref, bf16[8,2048]{1,0:T(8,128)(2,1)S(1)} %get-tuple-element.21.col_ref, bf16[8,2048]{1,0:T(8,128)(2,1)S(1)} %get-tuple-element.22.diff_ref, ...), custom_call_target="tpu_custom_call" | custom-call | tf_op jit(solution)/shard_map/pallas_call | solution.py:608
  9.2 5.9 %all-to-all-start = ((s16[8,8,2176]{2,1,0:T(8,128)(2,1)}), s16[8,8,2176]{2,1,0:T(8,128)(2,1)S(1)}, u32[]{:S(2)}, u32[]{:S(2)}) async-start(s16[8,8,2176]{2,1,0:T(8,128)(2,1)} %get-tuple-element.26), calls=%async_computation | async-start | bytes 557056 | tf_op jit(solution)/shard_map/all_to_all | solution.py:673
  15.2 0.7 %shard_map.102 = (bf16[2,128,2048]{2,1,0:T(8,128)(2,1)S(1)}, bf16[2,128,128]{2,1,0:T(8,128)(2,1)S(1)}, f32[8,128]{1,0:T(8,128)S(1)}) custom-call(f32[8,128]{1,0:T(8,128)S(1)} %get-tuple-element.28.sorted_ref), custom_call_target="tpu_custom_call" | custom-call | flops 2621440 | bytes 2097152 | tf_op jit(solution)/shard_map/pallas_call | solution.py:608
  15.8 8.2 %all-to-all-done.x_ref = s16[8,8,2176]{2,1,0:T(8,128)(2,1)S(1)} async-done(((s16[8,8,2176]{2,1,0:T(8,128)(2,1)}), s16[8,8,2176]{2,1,0:T(8,128)(2,1)S(1)}, u32[]{:S(2)}, u32[]{:S(2)}) %all-to-all-start) | async-done | bytes 278560 | tf_op jit(solution)/shard_map/all_to_all | solution.py:673
  24.1 2.1 %shard_map.103 = f32[1,8,2048]{2,1,0:T(8,128)} custom-call(s16[8,8,2176]{2,1,0:T(8,128)(2,1)S(1)} %all-to-all-done.x_ref, f32[8,2048]{1,0:T(8,128)S(1)} %get-tuple-element.27.field_ref, f32[8,128]{1,0:T(8,128)S(1)} %get-tuple-element.28.sorted_ref, f32[8,128]{1,0:T(8,128)S(1)} %get-tuple-element.29.noise_ref, ...), custom_call_target="tpu_custom_call" | custom-call | tf_op jit(solution)/shard_map/pallas_call | solution.py:608
Async XLA Ops:
  1.3 6.9 %collective-permute-start = (f32[8,1280]{1,0:T(8,128)S(1)}, f32[8,1280]{1,0:T(8,128)S(1)}, u32[]{:S(2)}, u32[]{:S(2)}) collective-permute-start(f32[8,1280]{1,0:T(8,128)S(1)} %get-tuple-element.23.down_ref), channel_id=1, source_target_pairs={{0,1},{1,2},{2,3},{3,0},{4,5},{5,6},{6,7},{7,4},{8,9},{9,10},{10,1... | collective-permute-start | bytes 122888 | tf_op jit(solution)/shard_map/ppermute | solution.py:656
  1.9 6.4 %collective-permute-start.1 = (f32[8,1280]{1,0:T(8,128)S(1)}, f32[8,1280]{1,0:T(8,128)S(1)}, u32[]{:S(2)}, u32[]{:S(2)}) collective-permute-start(f32[8,1280]{1,0:T(8,128)S(1)} %get-tuple-element.24.up_ref), channel_id=1, source_target_pairs={{0,3},{1,0},{2,1},{3,2},{4,7},{5,4},{6,5},{7,6},{8,11},{9,8},{10,9... | collective-permute-start | bytes 122888 | tf_op jit(solution)/shard_map/ppermute | solution.py:656
  3.9 4.4 %collective-permute-start.2 = (f32[8,512]{1,0:T(8,128)S(1)}, f32[8,512]{1,0:T(8,128)S(1)}, u32[]{:S(2)}, u32[]{:S(2)}) collective-permute-start(f32[8,512]{1,0:T(8,128)S(1)} %get-tuple-element.25.points_ref), channel_id=1, source_target_pairs={{0,2},{1,3},{2,0},{3,1},{4,6},{5,7},{6,4},{7,5},{8,10},{9,11},{10,... | collective-permute-start | bytes 49160 | tf_op jit(solution)/shard_map/ppermute | solution.py:656
  9.2 14.9 %all-to-all-start = ((s16[8,8,2176]{2,1,0:T(8,128)(2,1)}), s16[8,8,2176]{2,1,0:T(8,128)(2,1)S(1)}, u32[]{:S(2)}, u32[]{:S(2)}) async-start(s16[8,8,2176]{2,1,0:T(8,128)(2,1)} %get-tuple-element.26), calls=%async_computation | async-start | bytes 557056 | tf_op jit(solution)/shard_map/all_to_all | solution.py:673

commit v4 on v3

--- a/solution.py
+++ b/solution.py
@@ -207,8 +207,8 @@
     value_hbm,
     variance_hbm,
     noise_hbm,
-    down_ref,
-    up_ref,
+    pair_ref,
+    cross_ref,
     points_ref,
     partial_ref,
     sorted_ref,
@@ -321,16 +321,22 @@
     south = jnp.where(wide == SUBLANES - 1, 0.0, pltpu.roll(q, SUBLANES - 1, axis=0))
     partial = stencil(q, north, south, rate_row, rate_col, rate_diff)
     partial_ref[...] = partial
-    for ref, edge, missing in (
-        (down_ref, SUBLANES - 1, rate_diff - 0.5 * rate_row),
-        (up_ref, 0, rate_diff + 0.5 * rate_row),
-    ):
-        for n, array in enumerate((q, partial, missing)):
+    even = (me & 1) == 0
+    edges = [
+        (array[SUBLANES - 1 :, :], array[:1, :])
+        for array in (q, partial)
+    ] + [((rate_diff - 0.5 * rate_row)[SUBLANES - 1 :, :], (rate_diff + 0.5 * rate_row)[:1, :])]
+    for n, (lower, upper) in enumerate(edges):
+        for ref, row in (
+            (pair_ref, jnp.where(even, lower, upper)),
+            (cross_ref, jnp.where(even, upper, lower)),
+        ):
             for s in range(SUBLANES):
-                ref[s : s + 1, n * packed : (n + 1) * packed] = array[
-                    edge : edge + 1, s * packed : (s + 1) * packed
+                ref[s : s + 1, n * packed : (n + 1) * packed] = row[
+                    :, s * packed : (s + 1) * packed
                 ]
-        ref[:, 3 * packed :] = points_ref[...]
+    pair_ref[:, 3 * packed :] = points_ref[...]
+    cross_ref[:, 3 * packed :] = points_ref[...]
 
 
 def bell_of(dist, period, scale):
@@ -375,11 +381,11 @@
     row_ref,
     col_ref,
     diff_ref,
-    down_ref,
-    up_ref,
+    pair_ref,
+    cross_ref,
     points_ref,
-    above_ref,
-    below_ref,
+    paired_ref,
+    crossed_ref,
     far_ref,
     field_ref,
     out_ref,
@@ -395,12 +401,16 @@
     def section(ref, n):
         return ref[:, n * packed : (n + 1) * packed]
 
-    outer = (
-        section(above_ref, 0),
-        section(below_ref, 0),
-        section(above_ref, 1) + section(above_ref, 2) * section(up_ref, 0),
-        section(below_ref, 1) + section(below_ref, 2) * section(down_ref, 0),
-    )
+    def ahead(ref, sent_ref):
+        return section(ref, 0), section(ref, 1) + section(ref, 2) * section(sent_ref, 0)
+
+    even = (lax.axis_index("reg") & 1) == 0
+    paired, crossed = ahead(paired_ref, pair_ref), ahead(crossed_ref, cross_ref)
+    outer = [
+        jnp.where(even, one, other)
+        for x, y in zip(paired, crossed)
+        for one, other in ((y, x), (x, y))
+    ]
     for n, array in enumerate(outer):
         for s in range(SUBLANES):
             edge_ref[n : n + 1, s * packed : (s + 1) * packed] = array[s : s + 1, :]
@@ -418,7 +428,9 @@
     south = jnp.where(last, edge(3), pltpu.roll(field, SUBLANES - 1, axis=0))
     field = stencil(field, north, south, rate_row, rate_col, rate_diff)
 
-    points = points_ref[...] + far_ref[...] + above_ref[:, 3 * packed :] + below_ref[:, 3 * packed :]
+    points = (
+        points_ref[...] + far_ref[...] + paired_ref[:, 3 * packed :] + crossed_ref[:, 3 * packed :]
+    )
 
     def point(c):
         s, at = slot(c)
@@ -513,6 +525,7 @@
 
 def finish_kernel(
     sizes,
+    order,
     x_ref,
     field_ref,
     sorted_ref,
@@ -528,10 +541,11 @@
     me = lax.axis_index("mem")
     sub, lane = iota(0), iota(1)
     half = LANES // 2
+    place = [order.index(m) for m in range(members)]
     seen = jnp.zeros((SUBLANES, LANES), jnp.float32)
     steps = []
     for m in range(members):
-        tail = x_ref[m, :, columns:].astype(jnp.float32)
+        tail = x_ref[place[m], :, columns:].astype(jnp.float32)
         value = (row_of(tail, 0) + row_of(tail, 1) * SEEN_REST) * SEEN_UNIT
         seen = jnp.where(sub == m, value, seen)
         steps.append(row_of(tail, 2) * CODE_STEP)
@@ -581,7 +595,7 @@
         part = slice(begin, begin + CHUNK)
 
         def decoded(m, part=part):
-            return x_ref[m, :, part].astype(jnp.float32)
+            return x_ref[place[m], :, part].astype(jnp.float32)
 
         current = [decoded(m) * steps[m][:, :1] for m in range(members)]
         for m in range(members):
@@ -641,7 +655,7 @@
     rates = (courant_row, courant_column, diffusion)
     flat = [x.reshape(1, LANES) for x in (obs_owner, obs_cell, obs_order, obs_value, observation_variance)]
     operands = (prior_tracer_draws, *rates, *flat, obs_noise.T)
-    down, up, points, partial, table, noise, *rates = call(
+    pair, cross, points, partial, table, noise, *rates = call(
         functools.partial(start_kernel, sizes),
         [(message, f32), (message, f32), (points_shape, f32), (field, f32), (tile, f32), (tile, f32)]
         + [(x.shape, x.dtype) for x in rates],
@@ -652,12 +666,11 @@
         space=pltpu.HBM,
     )
 
-    def shifted(x, by):
-        return lax.ppermute(x, "reg", [(i, (i + by) % reg_count) for i in range(reg_count)])
-
-    above = shifted(down, 1)
-    below = shifted(up, -1)
-    far = [shifted(points, by) for by in range(2, reg_count - 1)]
+    pairs = [(i, i ^ 1) for i in range(reg_count)]
+    crosses = [(i, (i - 1 + 2 * (i & 1)) % reg_count) for i in range(reg_count)]
+    crossed = lax.ppermute(cross, "reg", crosses)
+    paired = lax.ppermute(pair, "reg", pairs)
+    far = lax.ppermute(points, "reg", [(i, i ^ 2) for i in range(reg_count)])
     col_taper, obs_taper, row_taper = call(
         functools.partial(taper_kernel, sizes),
         [((2, LANES, columns), jnp.bfloat16), ((2, LANES, LANES), jnp.bfloat16), (tile, f32)],
@@ -667,12 +680,17 @@
     forecast, send = call(
         functools.partial(middle_kernel, sizes),
         [(field, f32), ((mem_count, SUBLANES, columns + LANES), jnp.int16)],
-        (partial, *rates, down, up, points, above, below, sum(far[1:], far[0])),
+        (partial, *rates, pair, cross, points, paired, crossed, far),
         scratch=[pltpu.VMEM(field, f32)],
     )
-    slabs = lax.all_to_all(send, "mem", split_axis=0, concat_axis=0, tiled=True)
+    half = mem_count // 2
+    along = [*range(half // 2, -1, -1), *range(half // 2 + 1, half)]
+    order = [2 * z + y for y in range(2) for z in along]
+    slabs = lax.all_to_all(
+        send, "mem", split_axis=0, concat_axis=0, tiled=True, axis_index_groups=[order]
+    )
     (out,) = call(
-        functools.partial(finish_kernel, sizes),
+        functools.partial(finish_kernel, sizes, order),
         [(prior_tracer_draws.shape, f32)],
         (slabs, forecast, table, noise, col_taper, obs_taper, row_taper),
         scratch=[pltpu.VMEM((members, SUBLANES, CHUNK), f32)],
@@ -688,8 +706,7 @@
         members == 1
         and noise[1] == counts[0] == region_rows == SUBLANES
         and noise[0] == NOB * NBLK == LANES
-        and counts[1] >= 4
-        and counts[1] & (counts[1] - 1) == 0
+        and counts[1] == 4
         and columns % CHUNK == 0
         and columns & (columns - 1) == 0
     )

time: 26.5 us -> 23 us (0.87)
  waiting for transfers between devices: 10.4 us -> 8.01 us
  starting transfers between devices: 10.7 us -> 9.58 us
    all_to_all x1, waiting for transfers between devices: 8.23 us -> 4.31 us  [on_tile(): lax.all_to_all(send, 'mem', split_axis=0, concat_axis=0, tiled=True, axis...]
    ppermute x3, starting transfers between devices: 4.76 us -> 3.19 us  [the longest x1 2.59 us: on_tile(): crossed = lax.ppermute(cross, 'reg', crosses)]
    ppermute x3, waiting for transfers between devices: 2.16 us -> 3.7 us  [the longest x1 3.7 us: on_tile(): far = lax.ppermute(points, 'reg', [(i, i ^ 2) for i in range(reg_count)])]
    all_to_all x1, starting transfers between devices: 5.93 us -> 6.39 us  [on_tile(): lax.all_to_all(send, 'mem', split_axis=0, concat_axis=0, tiled=True, axis...]
where the time goes in v4:
time: 23 us; the launch traced here: 22.8 us
  starting transfers between devices  9.58 us (42%)
  waiting for transfers between devices  8.01 us (35%)
  Pallas kernels  5.16 us (22%)
    all_to_all x1, starting transfers between devices, on_tile(): lax.all_to_all(send, 'mem', split_axis=0, concat_axis=0, tiled=True, axis...  6.39 us
    pallas_call x4, Pallas kernels, call(): pl.pallas_call(kernel, out_shape=[jax.ShapeDtypeStruct(s, d) for s, d in...  5.16 us
    all_to_all x1, waiting for transfers between devices, on_tile(): lax.all_to_all(send, 'mem', split_axis=0, concat_axis=0, tiled=True, axis...  4.31 us
    ppermute x1, waiting for transfers between devices, on_tile(): far = lax.ppermute(points, 'reg', [(i, i ^ 2) for i in range(reg_count)])  3.7 us
    ppermute x1, starting transfers between devices, on_tile(): crossed = lax.ppermute(cross, 'reg', crosses)  2.59 us
    ppermute x1, starting transfers between devices, on_tile(): paired = lax.ppermute(pair, 'reg', pairs)  0.56 us
  transfers between devices with their start and end apart: 4, of which 2 were waited for; matrix products, arithmetic and copies ran while one was open for 0% of the time, Pallas kernels for 3%

profile of v4, /device:TPU:0, one launch (start us, length us, event | category | flops | bytes accessed | tf_op | source)
XLA Modules:
  0.0 22.8 jit_solution(4412386825455648325)
XLA Ops:
  0.0 1.4 %shard_map.100 = (f32[8,1280]{1,0:T(8,128)S(1)}, f32[8,1280]{1,0:T(8,128)S(1)}, f32[8,512]{1,0:T(8,128)S(1)}, f32[8,2048]{1,0:T(8,128)S(1)}, f32[8,128]{1,0:T(8,...) custom-call(f32[1,8,2048]{2,1,0:T(8,128)} %q_hbm.1, ...), custom_call_target="tpu_custom_call" | custom-call | tf_op jit(solution)/shard_map/pallas_call | solution.py:622
  1.4 0.6 %collective-permute-start = (f32[8,1280]{1,0:T(8,128)S(1)}, f32[8,1280]{1,0:T(8,128)S(1)}, u32[]{:S(2)}, u32[]{:S(2)}) collective-permute-start(f32[8,1280]{1,0:T(8,128)S(1)} %get-tuple-element.23.pair_ref), channel_id=1, source_target_pairs={{0,1},{1,0},{2,3},{3,2},{4,5},{5,4},{6,7},{7,6},{8,9},{9,8},{10,11... | collective-permute-start | bytes 122888 | tf_op jit(solution)/shard_map/ppermute | solution.py:672
  1.9 2.6 %collective-permute-start.1 = (f32[8,1280]{1,0:T(8,128)S(1)}, f32[8,1280]{1,0:T(8,128)S(1)}, u32[]{:S(2)}, u32[]{:S(2)}) collective-permute-start(f32[8,1280]{1,0:T(8,128)S(1)} %get-tuple-element.24.cross_ref), channel_id=1, source_target_pairs={{0,3},{1,2},{2,1},{3,0},{4,7},{5,6},{6,5},{7,4},{8,11},{9,10},{10,... | collective-permute-start | bytes 122888 | tf_op jit(solution)/shard_map/ppermute | solution.py:671
  4.5 0.0 collective-permute-start.2
  4.6 3.7 %collective-permute-done.2.far_ref = f32[8,512]{1,0:T(8,128)S(1)} collective-permute-done((f32[8,512]{1,0:T(8,128)S(1)}, f32[8,512]{1,0:T(8,128)S(1)}, u32[]{:S(2)}, u32[]{:S(2)}) %collective-permute-start.2) | collective-permute-done | bytes 16416 | tf_op jit(solution)/shard_map/ppermute | solution.py:673
  8.3 0.0 collective-permute-done.paired_ref
  8.3 0.0 collective-permute-done.1.crossed_ref
  8.3 0.9 %shard_map.101 = (f32[8,2048]{1,0:T(8,128)S(1)}, s16[8,8,2176]{2,1,0:T(8,128)(2,1)}) custom-call(f32[8,2048]{1,0:T(8,128)S(1)} %get-tuple-element.19.partial_ref, bf16[8,2048]{1,0:T(8,128)(2,1)S(1)} %get-tuple-element.20.row_ref, bf16[8,2048]{1,0:T(8,128)(2,1)S(1)} %get-tuple-element.21.col_ref, bf16[8,2048]{1,0:T(8,128)(2,1)S(1)} %get-tuple-element.22.diff_ref, ...), custom_call_target="tpu_custom_call" | custom-call | tf_op jit(solution)/shard_map/pallas_call | solution.py:622
  9.2 6.4 %all-to-all-start = ((s16[8,8,2176]{2,1,0:T(8,128)(2,1)}), s16[8,8,2176]{2,1,0:T(8,128)(2,1)S(1)}, u32[]{:S(2)}, u32[]{:S(2)}) async-start(s16[8,8,2176]{2,1,0:T(8,128)(2,1)} %get-tuple-element.26), calls=%async_computation | async-start | bytes 557056 | tf_op jit(solution)/shard_map/all_to_all | solution.py:689
  15.6 0.7 %shard_map.102 = (bf16[2,128,2048]{2,1,0:T(8,128)(2,1)S(1)}, bf16[2,128,128]{2,1,0:T(8,128)(2,1)S(1)}, f32[8,128]{1,0:T(8,128)S(1)}) custom-call(f32[8,128]{1,0:T(8,128)S(1)} %get-tuple-element.28.sorted_ref), custom_call_target="tpu_custom_call" | custom-call | flops 2621440 | bytes 2097152 | tf_op jit(solution)/shard_map/pallas_call | solution.py:622
  16.3 4.3 %all-to-all-done.x_ref = s16[8,8,2176]{2,1,0:T(8,128)(2,1)S(1)} async-done(((s16[8,8,2176]{2,1,0:T(8,128)(2,1)}), s16[8,8,2176]{2,1,0:T(8,128)(2,1)S(1)}, u32[]{:S(2)}, u32[]{:S(2)}) %all-to-all-start) | async-done | bytes 278560 | tf_op jit(solution)/shard_map/all_to_all | solution.py:689
  20.6 2.2 %shard_map.103 = f32[1,8,2048]{2,1,0:T(8,128)} custom-call(s16[8,8,2176]{2,1,0:T(8,128)(2,1)S(1)} %all-to-all-done.x_ref, f32[8,2048]{1,0:T(8,128)S(1)} %get-tuple-element.27.field_ref, f32[8,128]{1,0:T(8,128)S(1)} %get-tuple-element.28.sorted_ref, f32[8,128]{1,0:T(8,128)S(1)} %get-tuple-element.29.noise_ref, ...), custom_call_target="tpu_custom_call" | custom-call | tf_op jit(solution)/shard_map/pallas_call | solution.py:622
Async XLA Ops:
  1.4 6.9 %collective-permute-start = (f32[8,1280]{1,0:T(8,128)S(1)}, f32[8,1280]{1,0:T(8,128)S(1)}, u32[]{:S(2)}, u32[]{:S(2)}) collective-permute-start(f32[8,1280]{1,0:T(8,128)S(1)} %get-tuple-element.23.pair_ref), channel_id=1, source_target_pairs={{0,1},{1,0},{2,3},{3,2},{4,5},{5,4},{6,7},{7,6},{8,9},{9,8},{10,11... | collective-permute-start | bytes 122888 | tf_op jit(solution)/shard_map/ppermute | solution.py:672
  1.9 6.3 %collective-permute-start.1 = (f32[8,1280]{1,0:T(8,128)S(1)}, f32[8,1280]{1,0:T(8,128)S(1)}, u32[]{:S(2)}, u32[]{:S(2)}) collective-permute-start(f32[8,1280]{1,0:T(8,128)S(1)} %get-tuple-element.24.cross_ref), channel_id=1, source_target_pairs={{0,3},{1,2},{2,1},{3,0},{4,7},{5,6},{6,5},{7,4},{8,11},{9,10},{10,... | collective-permute-start | bytes 122888 | tf_op jit(solution)/shard_map/ppermute | solution.py:671
  4.5 3.7 %collective-permute-start.2 = (f32[8,512]{1,0:T(8,128)S(1)}, f32[8,512]{1,0:T(8,128)S(1)}, u32[]{:S(2)}, u32[]{:S(2)}) collective-permute-start(f32[8,512]{1,0:T(8,128)S(1)} %get-tuple-element.25.points_ref), channel_id=1, source_target_pairs={{0,2},{1,3},{2,0},{3,1},{4,6},{5,7},{6,4},{7,5},{8,10},{9,11},{10,... | collective-permute-start | bytes 49160 | tf_op jit(solution)/shard_map/ppermute | solution.py:673
  9.2 11.4 %all-to-all-start = ((s16[8,8,2176]{2,1,0:T(8,128)(2,1)}), s16[8,8,2176]{2,1,0:T(8,128)(2,1)S(1)}, u32[]{:S(2)}, u32[]{:S(2)}) async-start(s16[8,8,2176]{2,1,0:T(8,128)(2,1)} %get-tuple-element.26), calls=%async_computation | async-start | bytes 557056 | tf_op jit(solution)/shard_map/all_to_all | solution.py:689

commit v5 on v4

--- a/solution.py
+++ b/solution.py
@@ -383,12 +383,11 @@
     diff_ref,
     pair_ref,
     cross_ref,
-    points_ref,
     paired_ref,
     crossed_ref,
-    far_ref,
     field_ref,
-    out_ref,
+    code_ref,
+    steps_ref,
     edge_ref,
 ):
     reg_count, region_rows, slab_rows, columns = sizes
@@ -428,6 +427,18 @@
     south = jnp.where(last, edge(3), pltpu.roll(field, SUBLANES - 1, axis=0))
     field = stencil(field, north, south, rate_row, rate_col, rate_diff)
 
+    field_ref[...] = field
+    peak = jnp.max(jnp.max(jnp.abs(field), axis=1, keepdims=True), axis=0, keepdims=True)
+    steps = jnp.maximum(jnp.ceil(peak * (1.0 / (CODE_TOP * CODE_STEP))), 1.0)
+    code = jnp.round(field * (1.0 / (steps * CODE_STEP)))
+    code_ref[...] = code.astype(jnp.int32).astype(jnp.int16)
+    steps_ref[...] = jnp.broadcast_to(steps, (SUBLANES, LANES))
+
+
+def observe_kernel(
+    sizes, points_ref, paired_ref, crossed_ref, far_ref, code_ref, steps_ref, out_ref
+):
+    packed = sizes[-1] // SUBLANES
     points = (
         points_ref[...] + far_ref[...] + paired_ref[:, 3 * packed :] + crossed_ref[:, 3 * packed :]
     )
@@ -457,15 +468,9 @@
     seen = jnp.broadcast_to(at_point(q1, (0, 0)), (SUBLANES, LANES)) / SEEN_UNIT
     whole = jnp.round(seen)
     rest = jnp.round((seen - whole) / SEEN_REST)
-    field_ref[...] = field
-    peak = jnp.max(jnp.max(jnp.abs(field), axis=1, keepdims=True), axis=0, keepdims=True)
-    steps = jnp.maximum(jnp.ceil(peak * (1.0 / (CODE_TOP * CODE_STEP))), 1.0)
-    code = jnp.round(field * (1.0 / (steps * CODE_STEP)))
     sub = iota(0)
-    tail = jnp.where(
-        sub == 0, whole, jnp.where(sub == 1, rest, jnp.broadcast_to(steps, (SUBLANES, LANES)))
-    )
-    message = jnp.concatenate([code, tail], axis=1).astype(jnp.int32).astype(jnp.int16)
+    tail = jnp.where(sub == 0, whole, jnp.where(sub == 1, rest, steps_ref[...]))
+    message = jnp.concatenate([code_ref[...], tail.astype(jnp.int32).astype(jnp.int16)], axis=1)
     for d in range(out_ref.shape[0]):
         out_ref[d] = message
 
@@ -562,9 +567,10 @@
         gains, local = twice(gains, block), twice(anomaly, block)
         pairs = [row_of(local, a) * gains for a in range(members)]
         row_taper = twice(rows_ref[...], block)
+        used = pairs[: members - 1]
         if last:
             own = [
-                jnp.sum(jnp.where(sub == me, pair, 0.0), axis=0, keepdims=True) for pair in pairs
+                jnp.sum(jnp.where(sub == me, pair, 0.0), axis=0, keepdims=True) for pair in used
             ]
             lefts.append([row_taper * x for x in own])
         else:
@@ -575,21 +581,18 @@
             )
             for a in range(members):
                 seen = seen + row_of(anomaly, a) * moved[a * SUBLANES : (a + 1) * SUBLANES]
-            lefts.append([row_taper * row_of(pair, m) for pair in pairs for m in range(members)])
+            lefts.append([row_taper * row_of(pair, m) for pair in used for m in range(members)])
     lefts = [split(jnp.concatenate(x, axis=0)) for x in lefts]
 
-    def added(starts, centred, weights):
+    def added(starts, fields, weights):
+        apart = [x - fields[-1] for x in fields[:-1]]
         updated = []
         for n, total in enumerate(starts):
-            for a in range(members):
+            for a, x in enumerate(apart):
                 at = (a * len(starts) + n) * SUBLANES
-                total = total + centred[a] * weights[at : at + SUBLANES]
+                total = total + x * weights[at : at + SUBLANES]
             updated.append(total)
         return updated
-
-    def centre(fields):
-        mean = sum(fields[1:], fields[0]) * (1.0 / members)
-        return [x - mean for x in fields]
 
     for begin in range(0, columns, CHUNK):
         part = slice(begin, begin + CHUNK)
@@ -608,12 +611,12 @@
                 preferred_element_type=jnp.float32,
             )
             if block + 1 < NBLK:
-                current = added(current, centre(current), weights)
+                current = added(current, current, weights)
                 for m in range(members):
                     now_ref[m] = current[m]
             else:
                 own = now_ref[me] + (field_ref[:, part] - sent)
-                (own,) = added([own], centre(current), weights)
+                (own,) = added([own], current, weights)
                 out_ref[0, :, part] = own
 
 
@@ -677,11 +680,16 @@
         (table,),
         cost=pl.CostEstimate(flops=10 * LANES * columns, bytes_accessed=8 * LANES * columns, transcendentals=LANES * columns),
     )
-    forecast, send = call(
+    forecast, code, steps = call(
         functools.partial(middle_kernel, sizes),
-        [(field, f32), ((mem_count, SUBLANES, columns + LANES), jnp.int16)],
-        (partial, *rates, pair, cross, points, paired, crossed, far),
+        [(field, f32), (field, jnp.int16), (tile, f32)],
+        (partial, *rates, pair, cross, paired, crossed),
         scratch=[pltpu.VMEM(field, f32)],
+    )
+    (send,) = call(
+        functools.partial(observe_kernel, sizes),
+        [((mem_count, SUBLANES, columns + LANES), jnp.int16)],
+        (points, paired, crossed, far, code, steps),
     )
     half = mem_count // 2
     along = [*range(half // 2, -1, -1), *range(half // 2 + 1, half)]

time: 23 us -> 22.8 us (level)
    ppermute x1, waiting for transfers between devices: 3.7 us -> 1.65 us  [on_tile(): far = lax.ppermute(points, 'reg', [(i, i ^ 2) for i in range(reg_count)])]
    ppermute x1, waiting for transfers between devices: 0.01 us -> 1.81 us  [on_tile(): crossed = lax.ppermute(cross, 'reg', crosses)]
    pallas_call x4 -> x5, Pallas kernels: 5.16 us -> 5.13 us  [call(): pl.pallas_call(kernel, out_shape=[jax.ShapeDtypeStruct(s, d) for s, d in...]
  transfers between devices with their start and end apart: 4 -> 4, of which waited for: 2 -> 3; matrix products, arithmetic and copies ran while one was open for 0% -> 0% of each run, Pallas kernels for 3% -> 4%
where the time goes in v5:
time: 22.8 us; the launch traced here: 22.5 us
  starting transfers between devices  9.58 us (42%)
  waiting for transfers between devices  7.78 us (34%)
  Pallas kernels  5.13 us (22%)
    all_to_all x1, starting transfers between devices, on_tile(): lax.all_to_all(send, 'mem', split_axis=0, concat_axis=0, tiled=True, axis...  6.39 us
    pallas_call x5, Pallas kernels, call(): pl.pallas_call(kernel, out_shape=[jax.ShapeDtypeStruct(s, d) for s, d in...  5.13 us
    all_to_all x1, waiting for transfers between devices, on_tile(): lax.all_to_all(send, 'mem', split_axis=0, concat_axis=0, tiled=True, axis...  4.31 us
    ppermute x1, starting transfers between devices, on_tile(): crossed = lax.ppermute(cross, 'reg', crosses)  2.59 us
    ppermute x1, waiting for transfers between devices, on_tile(): crossed = lax.ppermute(cross, 'reg', crosses)  1.81 us
    ppermute x1, waiting for transfers between devices, on_tile(): far = lax.ppermute(points, 'reg', [(i, i ^ 2) for i in range(reg_count)])  1.65 us
    ppermute x1, starting transfers between devices, on_tile(): paired = lax.ppermute(pair, 'reg', pairs)  0.56 us
  transfers between devices with their start and end apart: 4, of which 3 were waited for; matrix products, arithmetic and copies ran while one was open for 0% of the time, Pallas kernels for 4%

profile of v5, /device:TPU:0, one launch (start us, length us, event | category | flops | bytes accessed | tf_op | source)
XLA Modules:
  0.0 22.5 jit_solution(15211806454223265048)
XLA Ops:
  0.0 1.4 %shard_map.100 = (f32[8,1280]{1,0:T(8,128)S(1)}, f32[8,1280]{1,0:T(8,128)S(1)}, f32[8,512]{1,0:T(8,128)S(1)}, f32[8,2048]{1,0:T(8,128)S(1)}, f32[8,128]{1,0:T(8,...) custom-call(f32[1,8,2048]{2,1,0:T(8,128)} %q_hbm.1, ...), custom_call_target="tpu_custom_call" | custom-call | tf_op jit(solution)/shard_map/pallas_call | solution.py:625
  1.4 0.6 %collective-permute-start = (f32[8,1280]{1,0:T(8,128)S(1)}, f32[8,1280]{1,0:T(8,128)S(1)}, u32[]{:S(2)}, u32[]{:S(2)}) collective-permute-start(f32[8,1280]{1,0:T(8,128)S(1)} %get-tuple-element.21.pair_ref), channel_id=1, source_target_pairs={{0,1},{1,0},{2,3},{3,2},{4,5},{5,4},{6,7},{7,6},{8,9},{9,8},{10,11... | collective-permute-start | bytes 122888 | tf_op jit(solution)/shard_map/ppermute | solution.py:675
  1.9 2.6 %collective-permute-start.1 = (f32[8,1280]{1,0:T(8,128)S(1)}, f32[8,1280]{1,0:T(8,128)S(1)}, u32[]{:S(2)}, u32[]{:S(2)}) collective-permute-start(f32[8,1280]{1,0:T(8,128)S(1)} %get-tuple-element.22.cross_ref), channel_id=1, source_target_pairs={{0,3},{1,2},{2,1},{3,0},{4,7},{5,6},{6,5},{7,4},{8,11},{9,10},{10,... | collective-permute-start | bytes 122888 | tf_op jit(solution)/shard_map/ppermute | solution.py:674
  4.5 0.0 collective-permute-start.2
  4.6 0.0 collective-permute-done.paired_ref
  4.6 1.8 %collective-permute-done.1.crossed_ref = f32[8,1280]{1,0:T(8,128)S(1)} collective-permute-done((f32[8,1280]{1,0:T(8,128)S(1)}, f32[8,1280]{1,0:T(8,128)S(1)}, u32[]{:S(2)}, u32[]{:S(2)}) %collective-permute-start.1) | collective-permute-done | bytes 40992 | tf_op jit(solution)/shard_map/ppermute | solution.py:674
  6.4 0.2 %shard_map.101 = (f32[8,2048]{1,0:T(8,128)S(1)}, s16[8,2048]{1,0:T(8,128)(2,1)S(1)}, f32[8,128]{1,0:T(8,128)S(1)}) custom-call(f32[8,2048]{1,0:T(8,128)S(1)} %get-tuple-element.23.partial_ref, bf16[8,2048]{1,0:T(8,128)(2,1)S(1)} %get-tuple-element.24.row_ref, bf16[8,2048]{1,0:T(8,128)(2,1)S(1)} %get-tuple-element.25.col_ref, ...), custom_call_target="tpu_custom_call" | custom-call | tf_op jit(solution)/shard_map/pallas_call | solution.py:625
  6.6 1.6 %collective-permute-done.2.far_ref = f32[8,512]{1,0:T(8,128)S(1)} collective-permute-done((f32[8,512]{1,0:T(8,128)S(1)}, f32[8,512]{1,0:T(8,128)S(1)}, u32[]{:S(2)}, u32[]{:S(2)}) %collective-permute-start.2) | collective-permute-done | bytes 16416 | tf_op jit(solution)/shard_map/ppermute | solution.py:676
  8.3 0.8 %shard_map.102 = s16[8,8,2176]{2,1,0:T(8,128)(2,1)} custom-call(f32[8,512]{1,0:T(8,128)S(1)} %get-tuple-element.20.points_ref, f32[8,1280]{1,0:T(8,128)S(1)} %collective-permute-done.paired_ref, f32[8,1280]{1,0:T(8,128)S(1)} %collective-permute-done.1.crossed_ref, f32[8,512]{1,0:T(8,128)S(1)} %collective-permute-done.2.far_ref, ...), custom_call_target="tpu_custom_call" | custom-call | tf_op jit(solution)/shard_map/pallas_call | solution.py:625
  9.0 6.4 %all-to-all-start = ((s16[8,8,2176]{2,1,0:T(8,128)(2,1)}), s16[8,8,2176]{2,1,0:T(8,128)(2,1)S(1)}, u32[]{:S(2)}, u32[]{:S(2)}) async-start(s16[8,8,2176]{2,1,0:T(8,128)(2,1)} %shard_map.102), calls=%async_computation | async-start | bytes 557056 | tf_op jit(solution)/shard_map/all_to_all | solution.py:697
  15.4 0.7 %shard_map.103 = (bf16[2,128,2048]{2,1,0:T(8,128)(2,1)S(1)}, bf16[2,128,128]{2,1,0:T(8,128)(2,1)S(1)}, f32[8,128]{1,0:T(8,128)S(1)}) custom-call(f32[8,128]{1,0:T(8,128)S(1)} %get-tuple-element.30.sorted_ref), custom_call_target="tpu_custom_call" | custom-call | flops 2621440 | bytes 2097152 | tf_op jit(solution)/shard_map/pallas_call | solution.py:625
  16.1 4.3 %all-to-all-done.x_ref = s16[8,8,2176]{2,1,0:T(8,128)(2,1)S(1)} async-done(((s16[8,8,2176]{2,1,0:T(8,128)(2,1)}), s16[8,8,2176]{2,1,0:T(8,128)(2,1)S(1)}, u32[]{:S(2)}, u32[]{:S(2)}) %all-to-all-start) | async-done | bytes 278560 | tf_op jit(solution)/shard_map/all_to_all | solution.py:697
  20.4 2.1 %shard_map.104 = f32[1,8,2048]{2,1,0:T(8,128)} custom-call(s16[8,8,2176]{2,1,0:T(8,128)(2,1)S(1)} %all-to-all-done.x_ref, f32[8,2048]{1,0:T(8,128)S(1)} %get-tuple-element.29.field_ref, f32[8,128]{1,0:T(8,128)S(1)} %get-tuple-element.30.sorted_ref, f32[8,128]{1,0:T(8,128)S(1)} %get-tuple-element.31.noise_ref, ...), custom_call_target="tpu_custom_call" | custom-call | tf_op jit(solution)/shard_map/pallas_call | solution.py:625
Async XLA Ops:
  1.4 3.2 %collective-permute-start = (f32[8,1280]{1,0:T(8,128)S(1)}, f32[8,1280]{1,0:T(8,128)S(1)}, u32[]{:S(2)}, u32[]{:S(2)}) collective-permute-start(f32[8,1280]{1,0:T(8,128)S(1)} %get-tuple-element.21.pair_ref), channel_id=1, source_target_pairs={{0,1},{1,0},{2,3},{3,2},{4,5},{5,4},{6,7},{7,6},{8,9},{9,8},{10,11... | collective-permute-start | bytes 122888 | tf_op jit(solution)/shard_map/ppermute | solution.py:675
  1.9 4.4 %collective-permute-start.1 = (f32[8,1280]{1,0:T(8,128)S(1)}, f32[8,1280]{1,0:T(8,128)S(1)}, u32[]{:S(2)}, u32[]{:S(2)}) collective-permute-start(f32[8,1280]{1,0:T(8,128)S(1)} %get-tuple-element.22.cross_ref), channel_id=1, source_target_pairs={{0,3},{1,2},{2,1},{3,0},{4,7},{5,6},{6,5},{7,4},{8,11},{9,10},{10,... | collective-permute-start | bytes 122888 | tf_op jit(solution)/shard_map/ppermute | solution.py:674
  4.5 3.7 %collective-permute-start.2 = (f32[8,512]{1,0:T(8,128)S(1)}, f32[8,512]{1,0:T(8,128)S(1)}, u32[]{:S(2)}, u32[]{:S(2)}) collective-permute-start(f32[8,512]{1,0:T(8,128)S(1)} %get-tuple-element.20.points_ref), channel_id=1, source_target_pairs={{0,2},{1,3},{2,0},{3,1},{4,6},{5,7},{6,4},{7,5},{8,10},{9,11},{10,... | collective-permute-start | bytes 49160 | tf_op jit(solution)/shard_map/ppermute | solution.py:676
  9.0 11.4 %all-to-all-start = ((s16[8,8,2176]{2,1,0:T(8,128)(2,1)}), s16[8,8,2176]{2,1,0:T(8,128)(2,1)S(1)}, u32[]{:S(2)}, u32[]{:S(2)}) async-start(s16[8,8,2176]{2,1,0:T(8,128)(2,1)} %shard_map.102), calls=%async_computation | async-start | bytes 557056 | tf_op jit(solution)/shard_map/all_to_all | solution.py:697

commit v6 on v5

--- a/solution.py
+++ b/solution.py
@@ -163,7 +163,6 @@
 POINTS = [(dr, dc) for dr in range(-2, 3) for dc in range(-2, 3) if abs(dr) + abs(dc) <= 2]
 CROSS = [(0, 0), (-1, 0), (1, 0), (0, -1), (0, 1)]
 TILES = -(-(len(POINTS) + 3 * len(CROSS)) // SUBLANES)
-CHUNK = 4 * LANES
 CODE_STEP = 2.0**-20
 CODE_TOP = 32767.0
 SEEN_UNIT = 2.0**-11
@@ -558,7 +557,20 @@
     observed = value + jnp.sqrt(variance) * noise_ref[...]
     inverse_variance = 1.0 / variance
     scale = 1.0 / (members - 1)
-    lefts = []
+    def added(starts, fields, weights):
+        apart = [x - fields[-1] for x in fields[:-1]]
+        updated = []
+        for n, total in enumerate(starts):
+            for a, x in enumerate(apart):
+                at = (a * len(starts) + n) * SUBLANES
+                total = total + x * weights[at : at + SUBLANES]
+            updated.append(total)
+        return updated
+
+    current = [x_ref[place[m], :, :columns].astype(jnp.float32) * steps[m][:, :1] for m in range(members)]
+    for m in range(members):
+        now_ref[m] = current[m]
+    base = field_ref[...] - now_ref[me]
     for block in range(NBLK):
         last = block + 1 == NBLK
         anomaly = seen - jnp.sum(seen, axis=0, keepdims=True) * (1.0 / members)
@@ -572,7 +584,7 @@
             own = [
                 jnp.sum(jnp.where(sub == me, pair, 0.0), axis=0, keepdims=True) for pair in used
             ]
-            lefts.append([row_taper * x for x in own])
+            left = [row_taper * x for x in own]
         else:
             moved = jnp.dot(
                 split(jnp.concatenate(pairs, axis=0)),
@@ -581,43 +593,18 @@
             )
             for a in range(members):
                 seen = seen + row_of(anomaly, a) * moved[a * SUBLANES : (a + 1) * SUBLANES]
-            lefts.append([row_taper * row_of(pair, m) for pair in used for m in range(members)])
-    lefts = [split(jnp.concatenate(x, axis=0)) for x in lefts]
-
-    def added(starts, fields, weights):
-        apart = [x - fields[-1] for x in fields[:-1]]
-        updated = []
-        for n, total in enumerate(starts):
-            for a, x in enumerate(apart):
-                at = (a * len(starts) + n) * SUBLANES
-                total = total + x * weights[at : at + SUBLANES]
-            updated.append(total)
-        return updated
-
-    for begin in range(0, columns, CHUNK):
-        part = slice(begin, begin + CHUNK)
-
-        def decoded(m, part=part):
-            return x_ref[place[m], :, part].astype(jnp.float32)
-
-        current = [decoded(m) * steps[m][:, :1] for m in range(members)]
-        for m in range(members):
-            now_ref[m] = current[m]
-        sent = now_ref[me]
-        for block in range(NBLK):
-            weights = jnp.dot(
-                lefts[block],
-                stacked(columns_ref, block, part),
-                preferred_element_type=jnp.float32,
-            )
-            if block + 1 < NBLK:
-                current = added(current, current, weights)
-                for m in range(members):
-                    now_ref[m] = current[m]
-            else:
-                own = now_ref[me] + (field_ref[:, part] - sent)
-                (own,) = added([own], current, weights)
-                out_ref[0, :, part] = own
+            left = [row_taper * row_of(pair, m) for pair in used for m in range(members)]
+        weights = jnp.dot(
+            split(jnp.concatenate(left, axis=0)),
+            stacked(columns_ref, block),
+            preferred_element_type=jnp.float32,
+        )
+        if last:
+            (out_ref[0],) = added([now_ref[me] + base], current, weights)
+        else:
+            current = added(current, current, weights)
+            for m in range(members):
+                now_ref[m] = current[m]
 
 
 def call(kernel, outs, args, scratch=(), cost=None, space=pltpu.VMEM):
@@ -701,7 +688,7 @@
         functools.partial(finish_kernel, sizes, order),
         [(prior_tracer_draws.shape, f32)],
         (slabs, forecast, table, noise, col_taper, obs_taper, row_taper),
-        scratch=[pltpu.VMEM((members, SUBLANES, CHUNK), f32)],
+        scratch=[pltpu.VMEM((members, *field), f32)],
     )
     return out
 
@@ -715,7 +702,7 @@
         and noise[1] == counts[0] == region_rows == SUBLANES
         and noise[0] == NOB * NBLK == LANES
         and counts[1] == 4
-        and columns % CHUNK == 0
+        and columns % (SUBLANES * LANES) == 0
         and columns & (columns - 1) == 0
     )
 

time: 22.8 us -> 22.4 us (0.982)
  Pallas kernels: 5.13 us -> 4.8 us
    pallas_call x5, Pallas kernels: 5.13 us -> 4.8 us  [call(): pl.pallas_call(kernel, out_shape=[jax.ShapeDtypeStruct(s, d) for s, d in...]
where the time goes in v6:
time: 22.4 us; the launch traced here: 22.2 us
  starting transfers between devices  9.58 us (43%)
  waiting for transfers between devices  7.78 us (35%)
  Pallas kernels  4.8 us (21%)
    all_to_all x1, starting transfers between devices, on_tile(): lax.all_to_all(send, 'mem', split_axis=0, concat_axis=0, tiled=True, axis...  6.39 us
    pallas_call x5, Pallas kernels, call(): pl.pallas_call(kernel, out_shape=[jax.ShapeDtypeStruct(s, d) for s, d in...  4.8 us
    all_to_all x1, waiting for transfers between devices, on_tile(): lax.all_to_all(send, 'mem', split_axis=0, concat_axis=0, tiled=True, axis...  4.31 us
    ppermute x1, starting transfers between devices, on_tile(): crossed = lax.ppermute(cross, 'reg', crosses)  2.59 us
    ppermute x1, waiting for transfers between devices, on_tile(): crossed = lax.ppermute(cross, 'reg', crosses)  1.81 us
    ppermute x1, waiting for transfers between devices, on_tile(): far = lax.ppermute(points, 'reg', [(i, i ^ 2) for i in range(reg_count)])  1.65 us
    ppermute x1, starting transfers between devices, on_tile(): paired = lax.ppermute(pair, 'reg', pairs)  0.56 us
  transfers between devices with their start and end apart: 4, of which 3 were waited for; matrix products, arithmetic and copies ran while one was open for 0% of the time, Pallas kernels for 4%

profile of v6, /device:TPU:0, one launch (start us, length us, event | category | flops | bytes accessed | tf_op | source)
XLA Modules:
  0.0 22.2 jit_solution(11853888793435150547)
XLA Ops:
  0.0 1.4 %shard_map.100 = (f32[8,1280]{1,0:T(8,128)S(1)}, f32[8,1280]{1,0:T(8,128)S(1)}, f32[8,512]{1,0:T(8,128)S(1)}, f32[8,2048]{1,0:T(8,128)S(1)}, f32[8,128]{1,0:T(8,...) custom-call(f32[1,8,2048]{2,1,0:T(8,128)} %q_hbm.1, ...), custom_call_target="tpu_custom_call" | custom-call | tf_op jit(solution)/shard_map/pallas_call | solution.py:612
  1.4 0.6 %collective-permute-start = (f32[8,1280]{1,0:T(8,128)S(1)}, f32[8,1280]{1,0:T(8,128)S(1)}, u32[]{:S(2)}, u32[]{:S(2)}) collective-permute-start(f32[8,1280]{1,0:T(8,128)S(1)} %get-tuple-element.21.pair_ref), channel_id=1, source_target_pairs={{0,1},{1,0},{2,3},{3,2},{4,5},{5,4},{6,7},{7,6},{8,9},{9,8},{10,11... | collective-permute-start | bytes 122888 | tf_op jit(solution)/shard_map/ppermute | solution.py:662
  1.9 2.6 %collective-permute-start.1 = (f32[8,1280]{1,0:T(8,128)S(1)}, f32[8,1280]{1,0:T(8,128)S(1)}, u32[]{:S(2)}, u32[]{:S(2)}) collective-permute-start(f32[8,1280]{1,0:T(8,128)S(1)} %get-tuple-element.22.cross_ref), channel_id=1, source_target_pairs={{0,3},{1,2},{2,1},{3,0},{4,7},{5,6},{6,5},{7,4},{8,11},{9,10},{10,... | collective-permute-start | bytes 122888 | tf_op jit(solution)/shard_map/ppermute | solution.py:661
  4.5 0.0 collective-permute-start.2
  4.6 0.0 collective-permute-done.paired_ref
  4.6 1.8 %collective-permute-done.1.crossed_ref = f32[8,1280]{1,0:T(8,128)S(1)} collective-permute-done((f32[8,1280]{1,0:T(8,128)S(1)}, f32[8,1280]{1,0:T(8,128)S(1)}, u32[]{:S(2)}, u32[]{:S(2)}) %collective-permute-start.1) | collective-permute-done | bytes 40992 | tf_op jit(solution)/shard_map/ppermute | solution.py:661
  6.4 0.2 %shard_map.101 = (f32[8,2048]{1,0:T(8,128)S(1)}, s16[8,2048]{1,0:T(8,128)(2,1)S(1)}, f32[8,128]{1,0:T(8,128)S(1)}) custom-call(f32[8,2048]{1,0:T(8,128)S(1)} %get-tuple-element.23.partial_ref, bf16[8,2048]{1,0:T(8,128)(2,1)S(1)} %get-tuple-element.24.row_ref, bf16[8,2048]{1,0:T(8,128)(2,1)S(1)} %get-tuple-element.25.col_ref, ...), custom_call_target="tpu_custom_call" | custom-call | tf_op jit(solution)/shard_map/pallas_call | solution.py:612
  6.6 1.6 %collective-permute-done.2.far_ref = f32[8,512]{1,0:T(8,128)S(1)} collective-permute-done((f32[8,512]{1,0:T(8,128)S(1)}, f32[8,512]{1,0:T(8,128)S(1)}, u32[]{:S(2)}, u32[]{:S(2)}) %collective-permute-start.2) | collective-permute-done | bytes 16416 | tf_op jit(solution)/shard_map/ppermute | solution.py:663
  8.3 0.8 %shard_map.102 = s16[8,8,2176]{2,1,0:T(8,128)(2,1)} custom-call(f32[8,512]{1,0:T(8,128)S(1)} %get-tuple-element.20.points_ref, f32[8,1280]{1,0:T(8,128)S(1)} %collective-permute-done.paired_ref, f32[8,1280]{1,0:T(8,128)S(1)} %collective-permute-done.1.crossed_ref, f32[8,512]{1,0:T(8,128)S(1)} %collective-permute-done.2.far_ref, ...), custom_call_target="tpu_custom_call" | custom-call | tf_op jit(solution)/shard_map/pallas_call | solution.py:612
  9.0 6.4 %all-to-all-start = ((s16[8,8,2176]{2,1,0:T(8,128)(2,1)}), s16[8,8,2176]{2,1,0:T(8,128)(2,1)S(1)}, u32[]{:S(2)}, u32[]{:S(2)}) async-start(s16[8,8,2176]{2,1,0:T(8,128)(2,1)} %shard_map.102), calls=%async_computation | async-start | bytes 557056 | tf_op jit(solution)/shard_map/all_to_all | solution.py:684
  15.4 0.7 %shard_map.103 = (bf16[2,128,2048]{2,1,0:T(8,128)(2,1)S(1)}, bf16[2,128,128]{2,1,0:T(8,128)(2,1)S(1)}, f32[8,128]{1,0:T(8,128)S(1)}) custom-call(f32[8,128]{1,0:T(8,128)S(1)} %get-tuple-element.30.sorted_ref), custom_call_target="tpu_custom_call" | custom-call | flops 2621440 | bytes 2097152 | tf_op jit(solution)/shard_map/pallas_call | solution.py:612
  16.1 4.3 %all-to-all-done.x_ref = s16[8,8,2176]{2,1,0:T(8,128)(2,1)S(1)} async-done(((s16[8,8,2176]{2,1,0:T(8,128)(2,1)}), s16[8,8,2176]{2,1,0:T(8,128)(2,1)S(1)}, u32[]{:S(2)}, u32[]{:S(2)}) %all-to-all-start) | async-done | bytes 278560 | tf_op jit(solution)/shard_map/all_to_all | solution.py:684
  20.4 1.8 %shard_map.104 = f32[1,8,2048]{2,1,0:T(8,128)} custom-call(s16[8,8,2176]{2,1,0:T(8,128)(2,1)S(1)} %all-to-all-done.x_ref, f32[8,2048]{1,0:T(8,128)S(1)} %get-tuple-element.29.field_ref, f32[8,128]{1,0:T(8,128)S(1)} %get-tuple-element.30.sorted_ref, f32[8,128]{1,0:T(8,128)S(1)} %get-tuple-element.31.noise_ref, ...), custom_call_target="tpu_custom_call" | custom-call | tf_op jit(solution)/shard_map/pallas_call | solution.py:612
Async XLA Ops:
  1.4 3.2 %collective-permute-start = (f32[8,1280]{1,0:T(8,128)S(1)}, f32[8,1280]{1,0:T(8,128)S(1)}, u32[]{:S(2)}, u32[]{:S(2)}) collective-permute-start(f32[8,1280]{1,0:T(8,128)S(1)} %get-tuple-element.21.pair_ref), channel_id=1, source_target_pairs={{0,1},{1,0},{2,3},{3,2},{4,5},{5,4},{6,7},{7,6},{8,9},{9,8},{10,11... | collective-permute-start | bytes 122888 | tf_op jit(solution)/shard_map/ppermute | solution.py:662
  1.9 4.4 %collective-permute-start.1 = (f32[8,1280]{1,0:T(8,128)S(1)}, f32[8,1280]{1,0:T(8,128)S(1)}, u32[]{:S(2)}, u32[]{:S(2)}) collective-permute-start(f32[8,1280]{1,0:T(8,128)S(1)} %get-tuple-element.22.cross_ref), channel_id=1, source_target_pairs={{0,3},{1,2},{2,1},{3,0},{4,7},{5,6},{6,5},{7,4},{8,11},{9,10},{10,... | collective-permute-start | bytes 122888 | tf_op jit(solution)/shard_map/ppermute | solution.py:661
  4.5 3.7 %collective-permute-start.2 = (f32[8,512]{1,0:T(8,128)S(1)}, f32[8,512]{1,0:T(8,128)S(1)}, u32[]{:S(2)}, u32[]{:S(2)}) collective-permute-start(f32[8,512]{1,0:T(8,128)S(1)} %get-tuple-element.20.points_ref), channel_id=1, source_target_pairs={{0,2},{1,3},{2,0},{3,1},{4,6},{5,7},{6,4},{7,5},{8,10},{9,11},{10,... | collective-permute-start | bytes 49160 | tf_op jit(solution)/shard_map/ppermute | solution.py:663
  9.0 11.4 %all-to-all-start = ((s16[8,8,2176]{2,1,0:T(8,128)(2,1)}), s16[8,8,2176]{2,1,0:T(8,128)(2,1)S(1)}, u32[]{:S(2)}, u32[]{:S(2)}) async-start(s16[8,8,2176]{2,1,0:T(8,128)(2,1)} %shard_map.102), calls=%async_computation | async-start | bytes 557056 | tf_op jit(solution)/shard_map/all_to_all | solution.py:684

commit v7 on v6

--- a/solution.py
+++ b/solution.py
@@ -568,9 +568,11 @@
         return updated
 
     current = [x_ref[place[m], :, :columns].astype(jnp.float32) * steps[m][:, :1] for m in range(members)]
-    for m in range(members):
-        now_ref[m] = current[m]
-    base = field_ref[...] - now_ref[me]
+    mine, my_step = place[0], steps[0]
+    for m in range(1, members):
+        mine = jnp.where(me == m, place[m], mine)
+        my_step = jnp.where(me == m, steps[m], my_step)
+    base = field_ref[...] - x_ref[mine, :, :columns].astype(jnp.float32) * my_step[:, :1]
     for block in range(NBLK):
         last = block + 1 == NBLK
         anomaly = seen - jnp.sum(seen, axis=0, keepdims=True) * (1.0 / members)

time: 22.4 us -> 22.4 us (level)
  no operation moved by 1% of the time
where the time goes in v7:
time: 22.4 us; the launch traced here: 22.2 us
  starting transfers between devices  9.58 us (43%)
  waiting for transfers between devices  7.78 us (35%)
  Pallas kernels  4.79 us (21%)
    all_to_all x1, starting transfers between devices, on_tile(): lax.all_to_all(send, 'mem', split_axis=0, concat_axis=0, tiled=True, axis...  6.39 us
    pallas_call x5, Pallas kernels, call(): pl.pallas_call(kernel, out_shape=[jax.ShapeDtypeStruct(s, d) for s, d in...  4.79 us
    all_to_all x1, waiting for transfers between devices, on_tile(): lax.all_to_all(send, 'mem', split_axis=0, concat_axis=0, tiled=True, axis...  4.31 us
    ppermute x1, starting transfers between devices, on_tile(): crossed = lax.ppermute(cross, 'reg', crosses)  2.59 us
    ppermute x1, waiting for transfers between devices, on_tile(): crossed = lax.ppermute(cross, 'reg', crosses)  1.81 us
    ppermute x1, waiting for transfers between devices, on_tile(): far = lax.ppermute(points, 'reg', [(i, i ^ 2) for i in range(reg_count)])  1.65 us
    ppermute x1, starting transfers between devices, on_tile(): paired = lax.ppermute(pair, 'reg', pairs)  0.56 us
  transfers between devices with their start and end apart: 4, of which 3 were waited for; matrix products, arithmetic and copies ran while one was open for 0% of the time, Pallas kernels for 4%

profile of v7, /device:TPU:0, one launch (start us, length us, event | category | flops | bytes accessed | tf_op | source)
XLA Modules:
  0.0 22.2 jit_solution(16991245025211989462)
XLA Ops:
  0.0 1.4 %shard_map.100 = (f32[8,1280]{1,0:T(8,128)S(1)}, f32[8,1280]{1,0:T(8,128)S(1)}, f32[8,512]{1,0:T(8,128)S(1)}, f32[8,2048]{1,0:T(8,128)S(1)}, f32[8,128]{1,0:T(8,...) custom-call(f32[1,8,2048]{2,1,0:T(8,128)} %q_hbm.1, ...), custom_call_target="tpu_custom_call" | custom-call | tf_op jit(solution)/shard_map/pallas_call | solution.py:614
  1.4 0.6 %collective-permute-start = (f32[8,1280]{1,0:T(8,128)S(1)}, f32[8,1280]{1,0:T(8,128)S(1)}, u32[]{:S(2)}, u32[]{:S(2)}) collective-permute-start(f32[8,1280]{1,0:T(8,128)S(1)} %get-tuple-element.21.pair_ref), channel_id=1, source_target_pairs={{0,1},{1,0},{2,3},{3,2},{4,5},{5,4},{6,7},{7,6},{8,9},{9,8},{10,11... | collective-permute-start | bytes 122888 | tf_op jit(solution)/shard_map/ppermute | solution.py:664
  1.9 2.6 %collective-permute-start.1 = (f32[8,1280]{1,0:T(8,128)S(1)}, f32[8,1280]{1,0:T(8,128)S(1)}, u32[]{:S(2)}, u32[]{:S(2)}) collective-permute-start(f32[8,1280]{1,0:T(8,128)S(1)} %get-tuple-element.22.cross_ref), channel_id=1, source_target_pairs={{0,3},{1,2},{2,1},{3,0},{4,7},{5,6},{6,5},{7,4},{8,11},{9,10},{10,... | collective-permute-start | bytes 122888 | tf_op jit(solution)/shard_map/ppermute | solution.py:663
  4.5 0.0 collective-permute-start.2
  4.6 0.0 collective-permute-done.paired_ref
  4.6 1.8 %collective-permute-done.1.crossed_ref = f32[8,1280]{1,0:T(8,128)S(1)} collective-permute-done((f32[8,1280]{1,0:T(8,128)S(1)}, f32[8,1280]{1,0:T(8,128)S(1)}, u32[]{:S(2)}, u32[]{:S(2)}) %collective-permute-start.1) | collective-permute-done | bytes 40992 | tf_op jit(solution)/shard_map/ppermute | solution.py:663
  6.4 0.2 %shard_map.101 = (f32[8,2048]{1,0:T(8,128)S(1)}, s16[8,2048]{1,0:T(8,128)(2,1)S(1)}, f32[8,128]{1,0:T(8,128)S(1)}) custom-call(f32[8,2048]{1,0:T(8,128)S(1)} %get-tuple-element.23.partial_ref, bf16[8,2048]{1,0:T(8,128)(2,1)S(1)} %get-tuple-element.24.row_ref, bf16[8,2048]{1,0:T(8,128)(2,1)S(1)} %get-tuple-element.25.col_ref, ...), custom_call_target="tpu_custom_call" | custom-call | tf_op jit(solution)/shard_map/pallas_call | solution.py:614
  6.6 1.6 %collective-permute-done.2.far_ref = f32[8,512]{1,0:T(8,128)S(1)} collective-permute-done((f32[8,512]{1,0:T(8,128)S(1)}, f32[8,512]{1,0:T(8,128)S(1)}, u32[]{:S(2)}, u32[]{:S(2)}) %collective-permute-start.2) | collective-permute-done | bytes 16416 | tf_op jit(solution)/shard_map/ppermute | solution.py:665
  8.3 0.8 %shard_map.102 = s16[8,8,2176]{2,1,0:T(8,128)(2,1)} custom-call(f32[8,512]{1,0:T(8,128)S(1)} %get-tuple-element.20.points_ref, f32[8,1280]{1,0:T(8,128)S(1)} %collective-permute-done.paired_ref, f32[8,1280]{1,0:T(8,128)S(1)} %collective-permute-done.1.crossed_ref, f32[8,512]{1,0:T(8,128)S(1)} %collective-permute-done.2.far_ref, ...), custom_call_target="tpu_custom_call" | custom-call | tf_op jit(solution)/shard_map/pallas_call | solution.py:614
  9.0 6.4 %all-to-all-start = ((s16[8,8,2176]{2,1,0:T(8,128)(2,1)}), s16[8,8,2176]{2,1,0:T(8,128)(2,1)S(1)}, u32[]{:S(2)}, u32[]{:S(2)}) async-start(s16[8,8,2176]{2,1,0:T(8,128)(2,1)} %shard_map.102), calls=%async_computation | async-start | bytes 557056 | tf_op jit(solution)/shard_map/all_to_all | solution.py:686
  15.4 0.7 %shard_map.103 = (bf16[2,128,2048]{2,1,0:T(8,128)(2,1)S(1)}, bf16[2,128,128]{2,1,0:T(8,128)(2,1)S(1)}, f32[8,128]{1,0:T(8,128)S(1)}) custom-call(f32[8,128]{1,0:T(8,128)S(1)} %get-tuple-element.30.sorted_ref), custom_call_target="tpu_custom_call" | custom-call | flops 2621440 | bytes 2097152 | tf_op jit(solution)/shard_map/pallas_call | solution.py:614
  16.1 4.3 %all-to-all-done.x_ref = s16[8,8,2176]{2,1,0:T(8,128)(2,1)S(1)} async-done(((s16[8,8,2176]{2,1,0:T(8,128)(2,1)}), s16[8,8,2176]{2,1,0:T(8,128)(2,1)S(1)}, u32[]{:S(2)}, u32[]{:S(2)}) %all-to-all-start) | async-done | bytes 278560 | tf_op jit(solution)/shard_map/all_to_all | solution.py:686
  20.4 1.8 %shard_map.104 = f32[1,8,2048]{2,1,0:T(8,128)} custom-call(s16[8,8,2176]{2,1,0:T(8,128)(2,1)S(1)} %all-to-all-done.x_ref, f32[8,2048]{1,0:T(8,128)S(1)} %get-tuple-element.29.field_ref, f32[8,128]{1,0:T(8,128)S(1)} %get-tuple-element.30.sorted_ref, f32[8,128]{1,0:T(8,128)S(1)} %get-tuple-element.31.noise_ref, ...), custom_call_target="tpu_custom_call" | custom-call | tf_op jit(solution)/shard_map/pallas_call | solution.py:614
Async XLA Ops:
  1.4 3.2 %collective-permute-start = (f32[8,1280]{1,0:T(8,128)S(1)}, f32[8,1280]{1,0:T(8,128)S(1)}, u32[]{:S(2)}, u32[]{:S(2)}) collective-permute-start(f32[8,1280]{1,0:T(8,128)S(1)} %get-tuple-element.21.pair_ref), channel_id=1, source_target_pairs={{0,1},{1,0},{2,3},{3,2},{4,5},{5,4},{6,7},{7,6},{8,9},{9,8},{10,11... | collective-permute-start | bytes 122888 | tf_op jit(solution)/shard_map/ppermute | solution.py:664
  1.9 4.4 %collective-permute-start.1 = (f32[8,1280]{1,0:T(8,128)S(1)}, f32[8,1280]{1,0:T(8,128)S(1)}, u32[]{:S(2)}, u32[]{:S(2)}) collective-permute-start(f32[8,1280]{1,0:T(8,128)S(1)} %get-tuple-element.22.cross_ref), channel_id=1, source_target_pairs={{0,3},{1,2},{2,1},{3,0},{4,7},{5,6},{6,5},{7,4},{8,11},{9,10},{10,... | collective-permute-start | bytes 122888 | tf_op jit(solution)/shard_map/ppermute | solution.py:663
  4.5 3.7 %collective-permute-start.2 = (f32[8,512]{1,0:T(8,128)S(1)}, f32[8,512]{1,0:T(8,128)S(1)}, u32[]{:S(2)}, u32[]{:S(2)}) collective-permute-start(f32[8,512]{1,0:T(8,128)S(1)} %get-tuple-element.20.points_ref), channel_id=1, source_target_pairs={{0,2},{1,3},{2,0},{3,1},{4,6},{5,7},{6,4},{7,5},{8,10},{9,11},{10,... | collective-permute-start | bytes 49160 | tf_op jit(solution)/shard_map/ppermute | solution.py:665
  9.0 11.4 %all-to-all-start = ((s16[8,8,2176]{2,1,0:T(8,128)(2,1)}), s16[8,8,2176]{2,1,0:T(8,128)(2,1)S(1)}, u32[]{:S(2)}, u32[]{:S(2)}) async-start(s16[8,8,2176]{2,1,0:T(8,128)(2,1)} %shard_map.102), calls=%async_computation | async-start | bytes 557056 | tf_op jit(solution)/shard_map/all_to_all | solution.py:686

commit v8 on v6

--- a/solution.py
+++ b/solution.py
@@ -435,7 +435,7 @@
 
 
 def observe_kernel(
-    sizes, points_ref, paired_ref, crossed_ref, far_ref, code_ref, steps_ref, out_ref
+    sizes, points_ref, paired_ref, crossed_ref, far_ref, code_ref, steps_ref, taper_ref, out_ref
 ):
     packed = sizes[-1] // SUBLANES
     points = (
@@ -676,11 +676,11 @@
     (send,) = call(
         functools.partial(observe_kernel, sizes),
         [((mem_count, SUBLANES, columns + LANES), jnp.int16)],
-        (points, paired, crossed, far, code, steps),
+        (points, paired, crossed, far, code, steps, row_taper),
     )
     half = mem_count // 2
     along = [*range(half // 2, -1, -1), *range(half // 2 + 1, half)]
-    order = [2 * z + y for y in range(2) for z in along]
+    order = [2 * z + 1 for z in along] + [2 * (-z % half) for z in range(half)]
     slabs = lax.all_to_all(
         send, "mem", split_axis=0, concat_axis=0, tiled=True, axis_index_groups=[order]
     )

time: 22.4 us -> 22.4 us (level)
  blocking collectives: 0 us -> 12.1 us
  starting transfers between devices: 9.58 us -> 3.19 us
  waiting for transfers between devices: 7.78 us -> 2.76 us
  Pallas kernels: 4.8 us -> 4.11 us
    all_to_all x0 -> x1, blocking collectives: none -> 12.1 us  [on_tile(): lax.all_to_all(send, 'mem', split_axis=0, concat_axis=0, tiled=True, axis...]
    all_to_all x1 -> x0, starting transfers between devices: 6.39 us -> none  [on_tile(): lax.all_to_all(send, 'mem', split_axis=0, concat_axis=0, tiled=True, axis...]
    all_to_all x1 -> x0, waiting for transfers between devices: 4.31 us -> none  [on_tile(): lax.all_to_all(send, 'mem', split_axis=0, concat_axis=0, tiled=True, axis...]
    ppermute x1, waiting for transfers between devices: 1.81 us -> 1.11 us  [on_tile(): crossed = lax.ppermute(cross, 'reg', crosses)]
    pallas_call x5, Pallas kernels: 4.8 us -> 4.11 us  [call(): pl.pallas_call(kernel, out_shape=[jax.ShapeDtypeStruct(s, d) for s, d in...]
  transfers between devices with their start and end apart: 4 -> 3, of which waited for: 3 -> 2; matrix products, arithmetic and copies ran while one was open for 0% -> 0% of each run, Pallas kernels for 4% -> 4%
where the time goes in v8:
time: 22.4 us; the launch traced here: 22.2 us
  blocking collectives  12.1 us (54%)
  Pallas kernels  4.11 us (18%)
  starting transfers between devices  3.19 us (14%)
  waiting for transfers between devices  2.76 us (12%)
    all_to_all x1, blocking collectives, on_tile(): lax.all_to_all(send, 'mem', split_axis=0, concat_axis=0, tiled=True, axis...  12.1 us
    pallas_call x5, Pallas kernels, call(): pl.pallas_call(kernel, out_shape=[jax.ShapeDtypeStruct(s, d) for s, d in...  4.11 us
    ppermute x1, starting transfers between devices, on_tile(): crossed = lax.ppermute(cross, 'reg', crosses)  2.59 us
    ppermute x1, waiting for transfers between devices, on_tile(): far = lax.ppermute(points, 'reg', [(i, i ^ 2) for i in range(reg_count)])  1.65 us
    ppermute x1, waiting for transfers between devices, on_tile(): crossed = lax.ppermute(cross, 'reg', crosses)  1.11 us
    ppermute x1, starting transfers between devices, on_tile(): paired = lax.ppermute(pair, 'reg', pairs)  0.56 us
  transfers between devices with their start and end apart: 3, of which 2 were waited for; matrix products, arithmetic and copies ran while one was open for 0% of the time, Pallas kernels for 4%

profile of v8, /device:TPU:0, one launch (start us, length us, event | category | flops | bytes accessed | tf_op | source)
XLA Modules:
  0.0 22.2 jit_solution(17916282443806728272)
XLA Ops:
  0.0 1.4 %shard_map.100 = (f32[8,1280]{1,0:T(8,128)S(1)}, f32[8,1280]{1,0:T(8,128)S(1)}, f32[8,512]{1,0:T(8,128)S(1)}, f32[8,2048]{1,0:T(8,128)S(1)}, f32[8,128]{1,0:T(8,...) custom-call(f32[1,8,2048]{2,1,0:T(8,128)} %q_hbm.1, ...), custom_call_target="tpu_custom_call" | custom-call | tf_op jit(solution)/shard_map/pallas_call | solution.py:612
  1.4 0.6 %collective-permute-start = (f32[8,1280]{1,0:T(8,128)S(1)}, f32[8,1280]{1,0:T(8,128)S(1)}, u32[]{:S(2)}, u32[]{:S(2)}) collective-permute-start(f32[8,1280]{1,0:T(8,128)S(1)} %get-tuple-element.21.pair_ref), channel_id=1, source_target_pairs={{0,1},{1,0},{2,3},{3,2},{4,5},{5,4},{6,7},{7,6},{8,9},{9,8},{10,11... | collective-permute-start | bytes 122888 | tf_op jit(solution)/shard_map/ppermute | solution.py:662
  1.9 2.6 %collective-permute-start.1 = (f32[8,1280]{1,0:T(8,128)S(1)}, f32[8,1280]{1,0:T(8,128)S(1)}, u32[]{:S(2)}, u32[]{:S(2)}) collective-permute-start(f32[8,1280]{1,0:T(8,128)S(1)} %get-tuple-element.22.cross_ref), channel_id=1, source_target_pairs={{0,3},{1,2},{2,1},{3,0},{4,7},{5,6},{6,5},{7,4},{8,11},{9,10},{10,... | collective-permute-start | bytes 122888 | tf_op jit(solution)/shard_map/ppermute | solution.py:661
  4.5 0.0 collective-permute-start.2
  4.6 0.7 %shard_map.102 = (bf16[2,128,2048]{2,1,0:T(8,128)(2,1)S(1)}, bf16[2,128,128]{2,1,0:T(8,128)(2,1)S(1)}, f32[8,128]{1,0:T(8,128)S(1)}) custom-call(f32[8,128]{1,0:T(8,128)S(1)} %get-tuple-element.29.sorted_ref), custom_call_target="tpu_custom_call" | custom-call | flops 2621440 | bytes 2097152 | tf_op jit(solution)/shard_map/pallas_call | solution.py:612
  5.3 0.0 collective-permute-done.paired_ref
  5.3 1.1 %collective-permute-done.1.crossed_ref = f32[8,1280]{1,0:T(8,128)S(1)} collective-permute-done((f32[8,1280]{1,0:T(8,128)S(1)}, f32[8,1280]{1,0:T(8,128)S(1)}, u32[]{:S(2)}, u32[]{:S(2)}) %collective-permute-start.1) | collective-permute-done | bytes 40992 | tf_op jit(solution)/shard_map/ppermute | solution.py:661
  6.4 0.2 %shard_map.101 = (f32[8,2048]{1,0:T(8,128)S(1)}, s16[8,2048]{1,0:T(8,128)(2,1)S(1)}, f32[8,128]{1,0:T(8,128)S(1)}) custom-call(f32[8,2048]{1,0:T(8,128)S(1)} %get-tuple-element.23.partial_ref, bf16[8,2048]{1,0:T(8,128)(2,1)S(1)} %get-tuple-element.24.row_ref, bf16[8,2048]{1,0:T(8,128)(2,1)S(1)} %get-tuple-element.25.col_ref, ...), custom_call_target="tpu_custom_call" | custom-call | tf_op jit(solution)/shard_map/pallas_call | solution.py:612
  6.6 1.6 %collective-permute-done.2.far_ref = f32[8,512]{1,0:T(8,128)S(1)} collective-permute-done((f32[8,512]{1,0:T(8,128)S(1)}, f32[8,512]{1,0:T(8,128)S(1)}, u32[]{:S(2)}, u32[]{:S(2)}) %collective-permute-start.2) | collective-permute-done | bytes 16416 | tf_op jit(solution)/shard_map/ppermute | solution.py:663
  8.3 12.1 %all_to_all.5.x_ref = s16[8,8,2176]{2,1,0:T(8,128)(2,1)S(1)} all-to-all(s16[8,8,2176]{2,1,0:T(8,128)(2,1)S(1)} %shard_map.103), channel_id=1, replica_groups={{20,12,4,28,0,24,16,8},{21,13,5,29,1,25,17,9},{22,14,6,30,2,26,18,10},{..., dimensions={0} | all-to-all | bytes 557056 | tf_op jit(solution)/shard_map/all_to_all | solution.py:684
  20.5 1.8 %shard_map.104 = f32[1,8,2048]{2,1,0:T(8,128)} custom-call(s16[8,8,2176]{2,1,0:T(8,128)(2,1)S(1)} %all_to_all.5.x_ref, f32[8,2048]{1,0:T(8,128)S(1)} %get-tuple-element.31.field_ref, f32[8,128]{1,0:T(8,128)S(1)} %get-tuple-element.29.sorted_ref, f32[8,128]{1,0:T(8,128)S(1)} %get-tuple-element.32.noise_ref, ...), custom_call_target="tpu_custom_call" | custom-call | tf_op jit(solution)/shard_map/pallas_call | solution.py:612
  (1 shorter events, 0.0 us)
Async XLA Ops:
  1.4 3.9 %collective-permute-start = (f32[8,1280]{1,0:T(8,128)S(1)}, f32[8,1280]{1,0:T(8,128)S(1)}, u32[]{:S(2)}, u32[]{:S(2)}) collective-permute-start(f32[8,1280]{1,0:T(8,128)S(1)} %get-tuple-element.21.pair_ref), channel_id=1, source_target_pairs={{0,1},{1,0},{2,3},{3,2},{4,5},{5,4},{6,7},{7,6},{8,9},{9,8},{10,11... | collective-permute-start | bytes 122888 | tf_op jit(solution)/shard_map/ppermute | solution.py:662
  1.9 4.4 %collective-permute-start.1 = (f32[8,1280]{1,0:T(8,128)S(1)}, f32[8,1280]{1,0:T(8,128)S(1)}, u32[]{:S(2)}, u32[]{:S(2)}) collective-permute-start(f32[8,1280]{1,0:T(8,128)S(1)} %get-tuple-element.22.cross_ref), channel_id=1, source_target_pairs={{0,3},{1,2},{2,1},{3,0},{4,7},{5,6},{6,5},{7,4},{8,11},{9,10},{10,... | collective-permute-start | bytes 122888 | tf_op jit(solution)/shard_map/ppermute | solution.py:661
  4.5 3.7 %collective-permute-start.2 = (f32[8,512]{1,0:T(8,128)S(1)}, f32[8,512]{1,0:T(8,128)S(1)}, u32[]{:S(2)}, u32[]{:S(2)}) collective-permute-start(f32[8,512]{1,0:T(8,128)S(1)} %get-tuple-element.20.points_ref), channel_id=1, source_target_pairs={{0,2},{1,3},{2,0},{3,1},{4,6},{5,7},{6,4},{7,5},{8,10},{9,11},{10,... | collective-permute-start | bytes 49160 | tf_op jit(solution)/shard_map/ppermute | solution.py:663
